TPU v7x, 128 devices: a whole 4x4x4 slice. The times are simulated.
128 devices in a mesh: lat: 16 (over y, x), lon: 8 (over z, core).
Axes of the slice: x: 4, y: 4, z: 4, core: 2. Of those that a mesh axis runs over, the one named last changes fastest.
Arguments:
- gaussian_thermal_state: float32 [16, 1280, 2560], P(None, 'lat', 'lon'), may hold values from -6 to 6
- radiation_holder_device: int32 [128, 6400, 1], P(('lat', 'lon')), may hold values from 0 to 127; in each aligned block of 6400 rows (0 to 6399, 6400 to 12799, ..., all dimensions but the last counted through in order) at most 80 rows name the same one
- layer_opacity_depths: bfloat16 [128, 16, 16, 10240], P(('lat', 'lon')), may hold values from 0.049804688 to 3
- wavenumber_duos_placed: int32 [640], replicated, may hold values from 0 to 639, each once
- reduced_grid_sites: int32 [1280], P('lat'), may hold values from 640 to 2560
- weighted_polynomial_basis: bfloat16 [640, 1280, 1344], P(('lat', 'lon')), may hold values from -0.15625 to 0.15625
Outputs:
- new_temperature: float32 [16, 1280, 2560], P(None, 'lat', 'lon')
Inputs may be any that keep to these rules, and one draw needn't show every extreme that they name: `radiation_holder_device`: in each block d no owner is named by more than 80 of the block's 6400 columns; some owner is named by exactly 80 in some blocks. `wavenumber_duos_placed`: each pair number appears in exactly one slot.
All inputs are finite; a program needn't handle non-finite values.
Results may differ from a plain program's by a relative error of at most 0.0072.
Values may be sent and summed in bfloat16 or wider, within the bound.
No kernel may reach another device: no remote copies, remote signals or barrier semaphores. Data moves between devices by JAX's collectives and lax.ppermute only.
A program may use at most 192 MiB of HBM per device.

v0:
```python
import functools
import math

import jax
import jax.numpy as jnp
from jax import lax
from jax.experimental import pallas as pl
from jax.experimental.pallas import tpu as pltpu
from jax.sharding import PartitionSpec as P


DIFFUSION = 4.0
BF16 = jnp.bfloat16
F32 = jnp.float32
I32 = jnp.int32
ALL = ("lat", "lon")
NT = (((1,), (1,)), ((), ()))


def iota(shape, dim):
    return lax.broadcasted_iota(I32, shape, dim)


def mm(a, b):
    return jnp.dot(a, b, preferred_element_type=F32)


def split_mm_right(x, b):
    hi = x.astype(BF16)
    lo = (x - hi.astype(F32)).astype(BF16)
    return mm(hi, b) + mm(lo, b)


def pack_kernel(state_ref, owner_ref, out_ref, code_ref, halves, coarse, marks, owners, values, total):
    levels, lines, width = state_ref.shape
    rows, lanes = owner_ref.shape
    devices = 128
    low = 16
    high = out_ref.shape[0] // devices
    pool_x = (iota((width, lanes), 0) // 2 == iota((width, lanes), 1)).astype(F32).astype(BF16)
    summed = split_mm_right(state_ref[...].reshape(levels * lines, width), pool_x)
    for t in range(2):
        halves[t] = summed[:, t * 128 : (t + 1) * 128]
    for level in range(levels):
        for t in range(2):
            even = halves[t, pl.ds(level * lines, rows, stride=2), :]
            odd = halves[t, pl.ds(level * lines + 1, rows, stride=2), :]
            mean = 0.25 * (even + odd)
            coarse[level, :, t * 128 : (t + 1) * 128] = mean.astype(BF16).astype(F32)
    before = (iota((lanes, lanes), 0) < iota((lanes, lanes), 1)).astype(F32).astype(BF16)
    total[...] = jnp.zeros_like(total)
    short = iota((8, 128), 1) < 32

    def tails(x):
        moved = x
        for i in range(1, 4):
            moved = jnp.where(iota((8, 128), 0) % 4 == i, pltpu.roll(x, 32 * i, 1), moved)
        return [jnp.sum(moved[4 * i : 4 * i + 4, :], axis=0, keepdims=True) for i in range(2)]

    def chunk(c, base):
        start = pl.multiple_of(c * 8, 8)
        owner8 = owner_ref[pl.ds(start, 8), :]
        for u in range(8):
            match = (iota((devices, lanes), 0) == owner8[u : u + 1, :]).astype(F32)
            marks[u * devices : (u + 1) * devices, :] = match.astype(BF16)
        counted = mm(marks[...], before)
        ranks = []
        for u in range(8):
            here = counted[u * devices : (u + 1) * devices, :]
            match = (iota((devices, lanes), 0) == owner8[u : u + 1, :]).astype(F32)
            both = jnp.concatenate([base, base], axis=1)
            ranks.append(jnp.sum(match * (here + both), axis=0, keepdims=True))
            base = base + here[:, lanes - 1 : lanes]
        code = owner8 * 128 + jnp.concatenate(ranks, axis=0).astype(I32)
        ends = tails(jnp.where(short, code[:, 128:], 0))
        for i in range(2):
            code_ref[2 * c + i] = jnp.concatenate(
                [code[4 * i : 4 * i + 4, :128], ends[i], jnp.zeros((3, 128), I32)], axis=0
            )
        lines8 = [code[u : u + 1, :128] for u in range(8)] + ends
        temps = []
        for level in range(levels):
            block = coarse[level, pl.ds(start, 8), :]
            temps.append([block[u : u + 1, :128] for u in range(8)] + tails(block[:, 128:]))
        for u in range(10):
            span = slice(u * 128, (u + 1) * 128)
            owner = lines8[u] // 128
            rank = lines8[u] % 128
            match = (iota((devices, 128), 0) == owner).astype(F32)
            for h in range(high):
                part = ((rank // low) == h).astype(F32)
                owners[h * devices : (h + 1) * devices, span] = (match * part).astype(BF16)
            slot = (iota((low, 128), 0) == rank % low).astype(F32)
            for level in range(levels):
                values[level * low : (level + 1) * low, span] = (
                    slot * temps[level][u]
                ).astype(BF16)
        total[...] += lax.dot_general(
            owners[...], values[...], NT, preferred_element_type=F32
        )
        return base

    lax.fori_loop(0, rows // 8, chunk, jnp.zeros((devices, devices), F32))
    out_ref[...] = total[...].astype(BF16)


def pack(state, owner):
    levels, lines, _ = state.shape
    rows, lanes = owner.shape
    return pl.pallas_call(
        pack_kernel,
        out_shape=(
            jax.ShapeDtypeStruct((640, levels * 16), BF16),
            jax.ShapeDtypeStruct((rows // 4, 8, 128), I32),
        ),
        scratch_shapes=[
            pltpu.VMEM((2, levels * lines, 128), F32),
            pltpu.VMEM((levels, rows, lanes), F32),
            pltpu.VMEM((8 * 128, lanes), BF16),
            pltpu.VMEM((640, 1280), BF16),
            pltpu.VMEM((levels * 16, 1280), BF16),
            pltpu.VMEM((640, levels * 16), F32),
        ],
        compiler_params=pltpu.CompilerParams(vmem_limit_bytes=20 * 2**20),
        cost_estimate=pl.CostEstimate(flops=6 * 10**9, bytes_accessed=2 * 10**6, transcendentals=0),
        name="pack",
    )(state, owner)


def radiate_kernel(came_ref, depth_ref, out_ref, temp, lost, down, heat):
    blocks, levels, cap = came_ref.shape
    bands = depth_ref.shape[1]
    for j in range(blocks):
        temp[:, j * cap : (j + 1) * cap] = came_ref[j].astype(F32)
    temp[...] = jnp.exp(0.5 * temp[...])
    weight = (iota((bands, 1), 0).astype(F32) + 1.0) * (2.0 / (bands * (bands + 1)))
    flux = jnp.zeros((bands, blocks * cap), F32)
    for level in range(levels):
        share = 1.0 - jnp.exp(-depth_ref[level].astype(F32))
        lost[level] = share
        step = share * (flux - temp[level : level + 1, :])
        down[level] = step
        flux = flux - step
    flux = jnp.broadcast_to(temp[levels - 1 : levels, :], flux.shape)
    for level in reversed(range(levels)):
        step = lost[level] * (flux - temp[level : level + 1, :])
        flux = flux - step
        heat[level : level + 1, :] = jnp.sum(
            (step + down[level]) * weight, axis=0, keepdims=True
        )
    group = out_ref.shape[1]
    for b in range(levels // group):
        out_ref[b] = heat[b * group : (b + 1) * group, :].astype(BF16)


def radiate(came, depth, lat_size, lon_size):
    devices, levels, cap = came.shape
    bands = depth.shape[1]
    width = lon_size * cap
    group = levels // lon_size
    return pl.pallas_call(
        radiate_kernel,
        grid=(lat_size,),
        out_shape=jax.ShapeDtypeStruct((devices, group, width), BF16),
        in_specs=[
            pl.BlockSpec((lon_size, levels, cap), lambda a: (a, 0, 0)),
            pl.BlockSpec((levels, bands, width), lambda a: (0, 0, a)),
        ],
        out_specs=pl.BlockSpec((lon_size, group, width), lambda a: (a, 0, 0)),
        scratch_shapes=[
            pltpu.VMEM((levels, width), F32),
            pltpu.VMEM((levels, bands, width), F32),
            pltpu.VMEM((levels, bands, width), F32),
            pltpu.VMEM((levels, width), F32),
        ],
        compiler_params=pltpu.CompilerParams(vmem_limit_bytes=16 * 2**20),
        name="radiate",
    )(came, depth)


def turns(count, whole):
    quarter = jnp.floor(count * (4.0 / whole) + 0.5)
    angle = (count - quarter * (whole / 4.0)) * (2.0 * math.pi / whole)
    sq = angle * angle
    sin = angle * (1.0 + sq * (-1.0 / 6.0 + sq * (1.0 / 120.0 + sq * (-1.0 / 5040.0))))
    cos = 1.0 + sq * (-0.5 + sq * (1.0 / 24.0 + sq * (-1.0 / 720.0 + sq * (1.0 / 40320.0))))
    side = quarter.astype(I32) & 3
    odd = (side & 1) == 1
    real = jnp.where(odd, sin, cos)
    imag = jnp.where(odd, cos, sin)
    real = jnp.where((side == 1) | (side == 2), -real, real)
    imag = jnp.where(side >= 2, -imag, imag)
    return real, imag


def fine_kernel(nwave, pair_ref, fine_ref):
    devices = pair_ref.shape[1]
    nlon = fine_ref.shape[3]
    scale = 1.0 / math.sqrt(nlon)
    step_rows = 16
    lane = iota((step_rows, 128), 1).astype(F32)

    def block(i, carry):
        rows = pl.ds(pl.multiple_of(i * step_rows, step_rows), step_rows)
        for h in range(2):
            pair = pair_ref[0, rows, :].astype(F32)
            wave = pair if h == 0 else (nwave - 1.0) - pair
            wave = jnp.broadcast_to(wave, (step_rows, 128))
            c, s = turns(wave * lane, float(nlon))
            c, s = c * scale, s * scale
            rc, rs = turns(wave * 128.0, float(nlon))
            for t in range(nlon // 128):
                fine_ref[0, 2 * h, rows, t * 128 : (t + 1) * 128] = c.astype(BF16)
                fine_ref[0, 2 * h + 1, rows, t * 128 : (t + 1) * 128] = s.astype(BF16)
                c, s = c * rc - s * rs, s * rc + c * rs
        return carry

    lax.fori_loop(0, devices // step_rows, block, 0)


def coarse_kernel(nwave, pair_ref, coarse_ref):
    devices = pair_ref.shape[1]
    nlon = coarse_ref.shape[3] * 2
    scale = 1.0 / math.sqrt(nlon)
    step_rows = 16
    lane = iota((step_rows, 128), 1).astype(F32)
    lane_i = iota((step_rows, 128), 1)
    tail0 = ((lane_i // 32) * 160 + 128 + lane_i % 32).astype(F32)

    def block(i, carry):
        rows = pl.ds(pl.multiple_of(i * step_rows, step_rows), step_rows)
        for h in range(2):
            pair = pair_ref[0, rows, :].astype(F32)
            wave = pair if h == 0 else (nwave - 1.0) - pair
            wave = jnp.broadcast_to(wave, (step_rows, 128))
            amp, _ = turns(wave, 2.0 * nlon)
            amp = amp * (2.0 * scale)
            c, s = turns(wave * (4.0 * lane + 1.0), 2.0 * nlon)
            c, s = c * amp, s * amp
            rc, rs = turns(wave * 640.0, 2.0 * nlon)
            for t in range(8):
                coarse_ref[0, 2 * h, rows, t * 128 : (t + 1) * 128] = c.astype(BF16)
                coarse_ref[0, 2 * h + 1, rows, t * 128 : (t + 1) * 128] = s.astype(BF16)
                c, s = c * rc - s * rs, s * rc + c * rs
            c, s = turns(wave * (4.0 * tail0 + 1.0), 2.0 * nlon)
            c, s = c * amp, s * amp
            rc, rs = turns(wave * 2560.0, 2.0 * nlon)
            for t in range(8, 10):
                coarse_ref[0, 2 * h, rows, t * 128 : (t + 1) * 128] = c.astype(BF16)
                coarse_ref[0, 2 * h + 1, rows, t * 128 : (t + 1) * 128] = s.astype(BF16)
                c, s = c * rc - s * rs, s * rc + c * rs
        return carry

    lax.fori_loop(0, devices // step_rows, block, 0)


def table(kernel, pairs, nwave, width):
    group, devices, _ = pairs.shape
    size = group * 4 * devices * width
    return pl.pallas_call(
        functools.partial(kernel, nwave),
        grid=(group,),
        out_shape=pltpu.HBM((group, 4, devices, width), BF16),
        in_specs=[pl.BlockSpec((1, devices, 1), lambda s: (s, 0, 0))],
        out_specs=pl.BlockSpec((1, 4, devices, width), lambda s: (s, 0, 0, 0)),
        compiler_params=pltpu.CompilerParams(vmem_limit_bytes=8 * 2**20),
        cost_estimate=pl.CostEstimate(flops=10 * size, bytes_accessed=2 * size, transcendentals=0),
    )(pairs)


def fourier_kernel(piece_ref, fine_ref, out_ref, rows):
    blocks, group, lines, width = piece_ref.shape
    nlon = rows.shape[1]

    @pl.when(pl.program_id(0) == 0)
    def _():
        rows[...] = jnp.zeros_like(rows)
        for g in range(group):
            for j in range(blocks):
                rows[g * 128 : g * 128 + lines, j * width : (j + 1) * width] = piece_ref[j, g]

    out_ref[0] = lax.dot_general(
        fine_ref[0].reshape(out_ref.shape[1], nlon), rows[...], NT, preferred_element_type=F32
    )


def fourier(piece, fine):
    group, four, devices, nlon = fine.shape
    levels = piece.shape[1]
    return pl.pallas_call(
        fourier_kernel,
        grid=(group,),
        out_shape=jax.ShapeDtypeStruct((group, four * devices, levels * 128), F32),
        in_specs=[
            pl.BlockSpec(piece.shape, lambda s: (0, 0, 0, 0)),
            pl.BlockSpec((1, four, devices, nlon), lambda s: (s, 0, 0, 0)),
        ],
        out_specs=pl.BlockSpec((1, four * devices, levels * 128), lambda s: (s, 0, 0)),
        scratch_shapes=[pltpu.VMEM((levels * 128, nlon), BF16)],
        compiler_params=pltpu.CompilerParams(vmem_limit_bytes=16 * 2**20),
        name="fourier",
    )(piece, fine)


def unpack_kernel(came_ref, code_ref, out_ref, heat):
    blocks, groups = code_ref.shape[0], code_ref.shape[1]
    _, both, devices = came_ref.shape
    levels = 2
    cap = both // levels
    lines = heat.shape[1] // levels
    for j in range(blocks):

        def pick(g, carry):
            code = code_ref[j, g]
            owner = code // 128
            rank = code % 128
            marks = [
                (iota((devices, 128), 0) == owner[q : q + 1, :]).astype(F32).astype(BF16)
                for q in range(5)
            ]
            found = mm(came_ref[j], jnp.concatenate(marks, axis=1))
            for q in range(5):
                here = iota((cap, 128), 0) == rank[q : q + 1, :]
                for level in range(levels):
                    part = found[level * cap : (level + 1) * cap, q * 128 : (q + 1) * 128]
                    value = jnp.sum(jnp.where(here, part, 0.0), axis=0, keepdims=True)
                    if q < 4:
                        heat[j, pl.ds(level * lines + 4 * g + q, 1), :] = value
                    else:
                        tile = blocks + j // 4
                        mine = iota((1, 128), 1) // 32 == j % 4
                        for i in range(4):
                            moved = pltpu.roll(value, (32 * (j % 4 - i)) % 128, 1)
                            at = pl.ds(level * lines + 4 * g + i, 1)
                            heat[tile, at, :] = jnp.where(mine, moved, heat[tile, at, :])
            return carry

        lax.fori_loop(0, groups, pick, 0, unroll=2)
    for t in range(heat.shape[0]):
        out_ref[:, t * 128 : (t + 1) * 128] = heat[t].astype(BF16)


def unpack(came, code):
    blocks, groups = code.shape[0], code.shape[1]
    shape = (2 * groups * 4, blocks * 160)
    return pl.pallas_call(
        unpack_kernel,
        out_shape=jax.ShapeDtypeStruct(shape, BF16),
        scratch_shapes=[pltpu.VMEM((shape[1] // 128, shape[0], 128), F32)],
        compiler_params=pltpu.CompilerParams(vmem_limit_bytes=12 * 2**20),
        name="unpack",
    )(came, code)


def heated_kernel(nwave, heat_ref, coarse_ref, base_ref, pair_ref, sites_ref, out_ref, rows, mixed):
    step = pl.program_id(0)
    devices = pair_ref.shape[1]
    lines = heat_ref.shape[0] // 2
    cap = 80

    @pl.when(step == 0)
    def _():
        twice = iota((256, 2 * lines), 0)
        source = (twice // 128) * lines + (twice % 128) // 2
        keep = (source == iota((256, 2 * lines), 1)) & (twice % 128 < 2 * lines)
        rows[...] = mm(keep.astype(F32).astype(BF16), heat_ref[...]).astype(BF16)

    product = base_ref[0] + lax.dot_general(
        coarse_ref[0].reshape(4 * devices, rows.shape[1]),
        rows[...],
        NT,
        preferred_element_type=F32,
    )
    pair = pair_ref[0]
    for k in range(4):
        wave = pair if k < 2 else nwave - 1 - pair
        part = jnp.where(
            2 * wave < sites_ref[...], product[k * devices : (k + 1) * devices, :], 0.0
        )
        for level in range(2):
            mixed[pl.ds(level * 4 + k, devices, stride=8), :] = part[
                :, level * 128 : (level + 1) * 128
            ]
    for k in range(5):

        @pl.when(step == k)
        def _(k=k):
            out_ref[:, :, k * cap : (k + 1) * cap] = (
                mixed[...].reshape(devices, 8, 128)[:, :, :cap].astype(BF16)
            )


def heated(heat, coarse, base, pairs, sites, nwave):
    group, four, devices, half = coarse.shape
    return pl.pallas_call(
        functools.partial(heated_kernel, nwave),
        grid=(group,),
        out_shape=jax.ShapeDtypeStruct((devices, 8, group * 80), BF16),
        in_specs=[
            pl.BlockSpec(heat.shape, lambda s: (0, 0)),
            pl.BlockSpec((1, four, devices, half), lambda s: (s, 0, 0, 0)),
            pl.BlockSpec((1, four * devices, base.shape[2]), lambda s: (s, 0, 0)),
            pl.BlockSpec((1, devices, 1), lambda s: (s, 0, 0)),
            pl.BlockSpec(sites.shape, lambda s: (0, 0)),
        ],
        out_specs=pl.BlockSpec((devices, 8, group * 80), lambda s: (0, 0, 0)),
        scratch_shapes=[
            pltpu.VMEM((256, half), BF16),
            pltpu.VMEM((devices * 8, 128), F32),
        ],
        compiler_params=pltpu.CompilerParams(vmem_limit_bytes=16 * 2**20),
        name="heated",
    )(heat, coarse, base, pairs, sites)


def legendre_kernel(nwave, pair_ref, came_ref, basis_ref, out_ref, right):
    step = pl.program_id(0)
    ndeg, nlat = basis_ref.shape[1], basis_ref.shape[2]
    bands = nlat // 80
    for k in range(5):

        @pl.when(step == k)
        def _(k=k):
            for a in range(bands):
                block = came_ref[a * 8 : (a + 1) * 8, :, k * 80 : (k + 1) * 80].astype(F32)
                right[:, a * 80 : (a + 1) * 80] = block.reshape(64, 80).astype(BF16)

    pair = pair_ref[step]
    full = lax.dot_general(right[...], basis_ref[0], NT, preferred_element_type=F32)
    coeff = iota((64, ndeg), 1)
    head = (iota((64, ndeg), 0) % 4) < 2
    first = coeff < nwave - pair
    degree = jnp.where(first, pair + coeff, coeff - 1).astype(F32)
    factor = 1.0 / (1.0 + DIFFUSION * degree * (degree + 1.0) / (nwave * nwave))
    keep = (first & head) | (jnp.logical_not(first) & jnp.logical_not(head) & (coeff <= nwave))
    damped = jnp.where(keep, full * factor, 0.0).astype(BF16)
    synth = mm(damped, basis_ref[0])
    for k in range(5):

        @pl.when(step == k)
        def _(k=k):
            for a in range(bands):
                block = synth[:, a * 80 : (a + 1) * 80].reshape(8, 8, 80)
                out_ref[a * 8 : (a + 1) * 8, :, k * 80 : (k + 1) * 80] = block.astype(BF16)


def legendre(pairs, came, basis, nwave):
    group, ndeg, nlat = basis.shape
    return pl.pallas_call(
        functools.partial(legendre_kernel, nwave),
        grid_spec=pltpu.PrefetchScalarGridSpec(
            num_scalar_prefetch=1,
            grid=(group,),
            in_specs=[
                pl.BlockSpec(came.shape, lambda s, p: (0, 0, 0)),
                pl.BlockSpec((1, ndeg, nlat), lambda s, p: (s, 0, 0)),
            ],
            out_specs=pl.BlockSpec(came.shape, lambda s, p: (0, 0, 0)),
            scratch_shapes=[pltpu.VMEM((64, nlat), BF16)],
        ),
        out_shape=jax.ShapeDtypeStruct(came.shape, BF16),
        compiler_params=pltpu.CompilerParams(vmem_limit_bytes=24 * 2**20),
        name="legendre",
    )(pairs, came, basis)


def inverse_kernel(came_ref, fine_ref, out_ref, mixed, left, total):
    step = pl.program_id(0)
    devices = came_ref.shape[0]
    blocks, _, width = out_ref.shape
    for k in range(5):

        @pl.when(step == k)
        def _(k=k):
            mixed[:, :80] = (
                came_ref[:, :, k * 80 : (k + 1) * 80].astype(F32).reshape(devices * 8, 80)
            )

    for k in range(4):
        for level in range(2):
            part = mixed[pl.ds(level * 4 + k, devices, stride=8), :]
            left[level * 80 : (level + 1) * 80, k * devices : (k + 1) * devices] = part.T[
                :80, :
            ].astype(BF16)
    product = mm(left[...], fine_ref[0].reshape(4 * devices, total.shape[1]))

    @pl.when(step == 0)
    def _():
        total[...] = product

    @pl.when(step > 0)
    def _():
        total[...] += product

    @pl.when(step == pl.num_programs(0) - 1)
    def _():
        for j in range(blocks):
            out_ref[j] = total[:, j * width : (j + 1) * width].astype(BF16)


def inverse(came, fine, blocks):
    group, four, devices, nlon = fine.shape
    return pl.pallas_call(
        inverse_kernel,
        grid=(group,),
        out_shape=jax.ShapeDtypeStruct((blocks, 160, nlon // blocks), BF16),
        in_specs=[
            pl.BlockSpec(came.shape, lambda s: (0, 0, 0)),
            pl.BlockSpec((1, four, devices, nlon), lambda s: (s, 0, 0, 0)),
        ],
        out_specs=pl.BlockSpec((blocks, 160, nlon // blocks), lambda s: (0, 0, 0)),
        scratch_shapes=[
            pltpu.VMEM((devices * 8, 128), F32),
            pltpu.VMEM((160, four * devices), BF16),
            pltpu.VMEM((160, nlon), F32),
        ],
        compiler_params=pltpu.CompilerParams(vmem_limit_bytes=24 * 2**20),
        name="inverse",
    )(came, fine)


def in_hbm(x):
    return pltpu.with_memory_space_constraint(x, pltpu.HBM)


def swap(x, axes):
    return lax.all_to_all(x, axes, split_axis=0, concat_axis=0, tiled=True)


def per_device(state, holder, depths, pairs, sites, basis):
    levels, lines, width = state.shape
    group, _, _ = basis.shape
    nwave = pairs.shape[0] * 2
    nlon = nwave * 2
    lat_size = lax.axis_size("lat")
    lon_size = lax.axis_size("lon")
    devices = lat_size * lon_size
    level_group = levels // lon_size
    rows, cols = lines // 2, width // 2
    me = lax.axis_index("lat") * lon_size + lax.axis_index("lon")
    slots = pairs.reshape(devices, group).T[:, :, None]
    limits = jnp.pad(sites, (0, 128 - lines))
    limits = jnp.concatenate([limits, limits])[None, :]
    owner = jnp.pad(holder.reshape(rows, cols), ((0, 0), (0, 256 - cols)), constant_values=-1)

    piece = swap(state.astype(BF16), "lon").reshape(lon_size, level_group, lines, width)

    sorted_cols, code = pack(state, owner)
    outgoing = sorted_cols.reshape(5, devices, levels, 16).transpose(1, 2, 0, 3)
    came = swap(outgoing.reshape(devices, levels, 80), ALL)
    codes = swap(jnp.broadcast_to(code[None], (lon_size,) + code.shape), "lon")
    fine = table(fine_kernel, slots, nwave, nlon)
    heat = radiate(came, in_hbm(depths[0]), lat_size, lon_size)
    returned = swap(heat, ALL)
    coarse = table(coarse_kernel, slots, nwave, nlon // 2)
    base = fourier(piece, in_hbm(fine))
    returned = returned.reshape(devices, level_group, lon_size, 80).transpose(2, 1, 3, 0)
    warm = unpack(returned.reshape(lon_size, level_group * 80, devices), codes)
    sending = heated(warm, in_hbm(coarse), base, slots, limits, nwave)
    arrived = swap(sending, ALL)
    mine = lax.dynamic_slice_in_dim(pairs, me * group, group)
    spread = legendre(mine, arrived, in_hbm(basis.transpose(0, 2, 1)), nwave)
    back = swap(spread, ALL)
    grid = inverse(back, in_hbm(fine), lon_size)
    grid = swap(grid, "lon")
    return grid.reshape(levels, lines, width).astype(F32)


def solution(mesh):
    in_specs = (
        P(None, "lat", "lon"),
        P(("lat", "lon"), None, None),
        P(("lat", "lon"), None, None, None),
        P(),
        P("lat"),
        P(("lat", "lon"), None, None),
    )
    out_specs = P(None, "lat", "lon")
    return jax.shard_map(
        per_device, mesh=mesh, in_specs=in_specs, out_specs=out_specs, check_vma=False
    )
```

profile of v0, /device:TPU:1, one launch (start us, length us, event | category | flops | bytes accessed | tf_op | source)
XLA Modules:
  0.0 217.8 jit_solution(900632332999212897)
XLA Ops:
  0.0 0.8 reduce
  0.8 0.1 reshape.25
  0.9 1.5 copy-done
  2.5 8.1 %pack.1 = (bf16[640,256]{1,0:T(8,128)(2,1)S(1)}, s32[10,8,128]{2,1,0:T(8,128)S(1)}) custom-call(f32[16,80,320]{2,1,0:T(8,128)S(1)} %copy-done, s32[40,256]{1,0:T(8,128)S(1)} %pad.8.owner_ref), custom_call_target="tpu_custom_call" | custom-call | flops 6000000000 | bytes 2000000 | tf_op jit(solution)/shard_map/pack/pallas_call | solution.py:110
  10.6 0.2 copy.9
  10.8 0.4 reshape.26
  11.2 0.8 copy.10
  11.9 1.4 copy.11
  13.4 24.8 %all_to_all.35.came_ref = bf16[128,16,80]{2,1,0:T(8,128)(2,1)S(1)} all-to-all(bf16[128,16,80]{2,1,0:T(8,128)(2,1)S(1)} %copy.11), channel_id=1, replica_groups=mesh['lat'=16,'lon'=8] {'lat','lon'}, dimensions={0} | all-to-all | bytes 655360 | tf_op jit(solution)/shard_map/all_to_all | solution.py:527
  38.2 0.7 broadcast_in_dim.12
  38.9 4.5 %all-to-all-start.2 = ((s32[8,10,8,128]{3,2,1,0:T(8,128)}), s32[8,10,8,128]{3,2,1,0:T(8,128)S(1)}, u32[]{:S(2)}, u32[]{:S(2)}) async-start(s32[8,10,8,128]{3,2,1,0:T(8,128)} %broadcast_in_dim.12), calls=%async_computation.2 | async-start | bytes 655360 | tf_op jit(solution)/shard_map/all_to_all | solution.py:527
  43.5 13.0 %radiate.1 = bf16[128,2,640]{2,1,0:T(2,128)(2,1)} custom-call(bf16[128,16,80]{2,1,0:T(8,128)(2,1)S(1)} %all_to_all.35.came_ref, bf16[16,16,10240]{2,1,0:T(8,128)(2,1)} %bitcast.21), custom_call_target="tpu_custom_call" | custom-call | tf_op jit(solution)/shard_map/radiate/pallas_call | solution.py:161
  56.5 5.1 %all-to-all-start.1 = ((bf16[128,2,640]{2,1,0:T(2,128)(2,1)}), bf16[128,2,640]{2,1,0:T(2,128)(2,1)S(1)}, u32[]{:S(2)}, u32[]{:S(2)}) async-start(bf16[128,2,640]{2,1,0:T(2,128)(2,1)} %radiate.1), calls=%async_computation.1 | async-start | bytes 655360 | tf_op jit(solution)/shard_map/all_to_all | solution.py:527
  61.6 1.1 convert_element_type.9
  62.7 10.4 %all-to-all-done.1 = bf16[128,2,640]{2,1,0:T(2,128)(2,1)S(1)} async-done(((bf16[128,2,640]{2,1,0:T(2,128)(2,1)}), bf16[128,2,640]{2,1,0:T(2,128)(2,1)S(1)}, u32[]{:S(2)}, u32[]{:S(2)}) %all-to-all-start.1) | async-done | bytes 327712 | tf_op jit(solution)/shard_map/all_to_all | solution.py:527
  73.1 4.7 %all-to-all-start.3 = ((bf16[16,80,320]{2,1,0:T(8,128)(2,1)}), bf16[16,80,320]{2,1,0:T(8,128)(2,1)S(1)}, u32[]{:S(2)}, u32[]{:S(2)}) async-start(bf16[16,80,320]{2,1,0:T(8,128)(2,1)} %convert_element_type.9), calls=%async_computation.3 | async-start | bytes 1966080 | tf_op jit(solution)/shard_map/all_to_all | solution.py:527
  77.7 0.2 reshape.30
  77.9 1.0 copy.15.pair_ref
  79.0 9.6 %shard_map.64.coarse_ref = bf16[5,4,128,1280]{3,2,1,0:T(8,128)(2,1)} custom-call(s32[5,128,1]{2,1,0:T(8,128)S(1)} %copy.15.pair_ref), custom_call_target="tpu_custom_call" | custom-call | flops 32768000 | bytes 6553600 | tf_op jit(solution)/shard_map/pallas_call | solution.py:260
  88.6 10.0 %shard_map.65.fine_ref = bf16[5,4,128,2560]{3,2,1,0:T(8,128)(2,1)} custom-call(s32[5,128,1]{2,1,0:T(8,128)S(1)} %copy.15.pair_ref), custom_call_target="tpu_custom_call" | custom-call | flops 65536000 | bytes 13107200 | tf_op jit(solution)/shard_map/pallas_call | solution.py:260
  98.7 0.6 copy.12
  99.3 13.7 %unpack.1.heat_ref = bf16[80,1280]{1,0:T(8,128)(2,1)S(1)} custom-call(bf16[8,160,128]{2,1,0:T(8,128)(2,1)S(1)} %bitcast.18, s32[8,10,8,128]{3,2,1,0:T(8,128)S(1)} %all-to-all-done.2.code_ref), custom_call_target="tpu_custom_call" | custom-call | tf_op jit(solution)/shard_map/unpack/pallas_call | solution.py:346
  113.0 8.2 %fourier.1.base_ref = f32[5,512,256]{2,1,0:T(8,128)S(1)} custom-call(bf16[8,2,80,320]{3,2,1,0:T(8,128)(2,1)S(1)} %bitcast.17, bf16[5,4,128,2560]{3,2,1,0:T(8,128)(2,1)} %shard_map.65.fine_ref), custom_call_target="tpu_custom_call" | custom-call | tf_op jit(solution)/shard_map/fourier/pallas_call | solution.py:290
  121.2 7.4 %heated.1 = bf16[128,8,400]{2,1,0:T(8,128)(2,1)} custom-call(bf16[80,1280]{1,0:T(8,128)(2,1)S(1)} %unpack.1.heat_ref, bf16[5,4,128,1280]{3,2,1,0:T(8,128)(2,1)} %shard_map.64.coarse_ref, f32[5,512,256]{2,1,0:T(8,128)S(1)} %fourier.1.base_ref, s32[5,128,1]{2,1,0:T(8,128)S(1)} %copy.15.pair_ref, s32[1,256]{1,0:T(1,128)S(1)} %bitcast.19), custom_call_target="tpu_custom_call" | custom-call | tf_op jit(solution)/shard_map/heated/pallas_call | solution.py:395
  128.6 5.3 %all-to-all-start.4 = ((bf16[128,8,400]{2,1,0:T(8,128)(2,1)}), bf16[128,8,400]{2,1,0:T(8,128)(2,1)S(1)}, u32[]{:S(2)}, u32[]{:S(2)}) async-start(bf16[128,8,400]{2,1,0:T(8,128)(2,1)} %heated.1), calls=%async_computation.4 | async-start | bytes 2097152 | tf_op jit(solution)/shard_map/all_to_all | solution.py:527
  133.9 0.1 dynamic_slice.3.pair_ref
  134.0 18.9 %all-to-all-done.4.came_ref = bf16[128,8,400]{2,1,0:T(8,128)(2,1)S(1)} async-done(((bf16[128,8,400]{2,1,0:T(8,128)(2,1)}), bf16[128,8,400]{2,1,0:T(8,128)(2,1)S(1)}, u32[]{:S(2)}, u32[]{:S(2)}) %all-to-all-start.4) | async-done | bytes 819232 | tf_op jit(solution)/shard_map/all_to_all | solution.py:527
  152.9 13.7 %legendre.1 = bf16[128,8,400]{2,1,0:T(8,128)(2,1)S(1)} custom-call(s32[5]{0:T(128)S(1)} %dynamic_slice.3.pair_ref, bf16[128,8,400]{2,1,0:T(8,128)(2,1)S(1)} %all-to-all-done.4.came_ref, bf16[5,1344,1280]{2,1,0:T(8,128)(2,1)} %bitcast.20), custom_call_target="tpu_custom_call" | custom-call | tf_op jit(solution)/shard_map/legendre/pallas_call | solution.py:449
  166.6 23.4 %all_to_all.36.came_ref = bf16[128,8,400]{2,1,0:T(8,128)(2,1)S(1)} all-to-all(bf16[128,8,400]{2,1,0:T(8,128)(2,1)S(1)} %legendre.1), channel_id=1, replica_groups=mesh['lat'=16,'lon'=8] {'lat','lon'}, dimensions={0} | all-to-all | bytes 1638400 | tf_op jit(solution)/shard_map/all_to_all | solution.py:527
  190.0 8.3 %inverse.1 = bf16[8,160,320]{2,1,0:T(8,128)(2,1)S(1)} custom-call(bf16[128,8,400]{2,1,0:T(8,128)(2,1)S(1)} %all_to_all.36.came_ref, bf16[5,4,128,2560]{3,2,1,0:T(8,128)(2,1)} %shard_map.65.fine_ref), custom_call_target="tpu_custom_call" | custom-call | tf_op jit(solution)/shard_map/inverse/pallas_call | solution.py:503
  198.4 18.0 %all_to_all.37 = bf16[8,160,320]{2,1,0:T(8,128)(2,1)S(1)} all-to-all(bf16[8,160,320]{2,1,0:T(8,128)(2,1)S(1)} %inverse.1), channel_id=1, replica_groups=mesh['lat'=16,'lon'=8] {'lon'}, dimensions={0} | all-to-all | bytes 1638400 | tf_op jit(solution)/shard_map/all_to_all | solution.py:527
  216.4 1.4 convert.1
  (13 shorter events, 0.1 us)
Async XLA Ops:
  0.9 1.5 copy-start
  11.2 50.4 %copy-start.1 = (f32[16,80,320]{2,1,0:T(8,128)S(1)}, f32[16,80,320]{2,1,0:T(8,128)}, u32[]{:S(2)}) copy-start(f32[16,80,320]{2,1,0:T(8,128)} %state_ref.1) | copy-start | bytes 4915204
  38.9 17.6 %all-to-all-start.2 = ((s32[8,10,8,128]{3,2,1,0:T(8,128)}), s32[8,10,8,128]{3,2,1,0:T(8,128)S(1)}, u32[]{:S(2)}, u32[]{:S(2)}) async-start(s32[8,10,8,128]{3,2,1,0:T(8,128)} %broadcast_in_dim.12), calls=%async_computation.2 | async-start | bytes 655360 | tf_op jit(solution)/shard_map/all_to_all | solution.py:527
  43.5 34.2 %copy-start.3 = (s32[80]{0:T(128)S(1)}, s32[80]{0:T(128)}, u32[]{:S(2)}) copy-start(s32[80]{0:T(128)} %param.10) | copy-start | bytes 964
  43.5 34.2 %copy-start.2 = (s32[640]{0:T(1024)S(1)}, s32[640]{0:T(1024)}, u32[]{:S(2)}) copy-start(s32[640]{0:T(1024)} %param.9) | copy-start | bytes 7684
  56.5 16.5 %all-to-all-start.1 = ((bf16[128,2,640]{2,1,0:T(2,128)(2,1)}), bf16[128,2,640]{2,1,0:T(2,128)(2,1)S(1)}, u32[]{:S(2)}, u32[]{:S(2)}) async-start(bf16[128,2,640]{2,1,0:T(2,128)(2,1)} %radiate.1), calls=%async_computation.1 | async-start | bytes 655360 | tf_op jit(solution)/shard_map/all_to_all | solution.py:527
  73.1 39.9 %all-to-all-start.3 = ((bf16[16,80,320]{2,1,0:T(8,128)(2,1)}), bf16[16,80,320]{2,1,0:T(8,128)(2,1)S(1)}, u32[]{:S(2)}, u32[]{:S(2)}) async-start(bf16[16,80,320]{2,1,0:T(8,128)(2,1)} %convert_element_type.9), calls=%async_computation.3 | async-start | bytes 1966080 | tf_op jit(solution)/shard_map/all_to_all | solution.py:527
  128.6 24.3 %all-to-all-start.4 = ((bf16[128,8,400]{2,1,0:T(8,128)(2,1)}), bf16[128,8,400]{2,1,0:T(8,128)(2,1)S(1)}, u32[]{:S(2)}, u32[]{:S(2)}) async-start(bf16[128,8,400]{2,1,0:T(8,128)(2,1)} %heated.1), calls=%async_computation.4 | async-start | bytes 2097152 | tf_op jit(solution)/shard_map/all_to_all | solution.py:527
where the time goes:
time: 219 us; the launch traced here: 218 us
  Pallas kernels  92.1 us (42%)
  blocking collectives  66.2 us (30%)
  waiting for transfers between devices  29.3 us (13%)
  starting transfers between devices  19.5 us (9%)
  local copies, waits for them, and re-layouts  7.1 us (3%)
  other arithmetic  3.26 us (1%)
    all_to_all x3, blocking collectives, swap(): return lax.all_to_all(x, axes, split_axis=0, concat_axis=0, tiled=True)  66.2 us
    all_to_all x4, waiting for transfers between devices, swap(): return lax.all_to_all(x, axes, split_axis=0, concat_axis=0, tiled=True)  29.3 us
    pallas_call x2, Pallas kernels, table(): pl.pallas_call(functools.partial(kernel, nwave), grid=(group,), out_shape...  19.7 us
    all_to_all x4, starting transfers between devices, swap(): return lax.all_to_all(x, axes, split_axis=0, concat_axis=0, tiled=True)  19.5 us
    pallas_call x1, Pallas kernels, legendre(): pl.pallas_call(functools.partial(legendre_kernel, nwave), grid_spec=pltpu...  13.7 us
    pallas_call x1, Pallas kernels, unpack(): pl.pallas_call(unpack_kernel, out_shape=jax.ShapeDtypeStruct(shape, BF16)...  13.7 us
    pallas_call x1, Pallas kernels, radiate(): pl.pallas_call(radiate_kernel, grid=(lat_size,), out_shape=jax.ShapeDtype...  13 us
    pallas_call x1, Pallas kernels, inverse(): pl.pallas_call(inverse_kernel, grid=(group,), out_shape=jax.ShapeDtypeStr...  8.35 us
  transfers between devices with their start and end apart: 4, of which 2 were waited for; matrix products, arithmetic and copies ran while one was open for 1% of the time, Pallas kernels for 21%

commit v1 on v0

--- a/solution.py
+++ b/solution.py
@@ -193,12 +193,16 @@
     return real, imag
 
 
+def turned(c, s, rc, rs):
+    return c * rc - s * rs, s * rc + c * rs
+
+
 def fine_kernel(nwave, pair_ref, fine_ref):
     devices = pair_ref.shape[1]
     nlon = fine_ref.shape[3]
     scale = 1.0 / math.sqrt(nlon)
     step_rows = 16
-    lane = iota((step_rows, 128), 1).astype(F32)
+    lane = iota((step_rows, 128), 1)
 
     def block(i, carry):
         rows = pl.ds(pl.multiple_of(i * step_rows, step_rows), step_rows)
@@ -206,49 +210,30 @@
             pair = pair_ref[0, rows, :].astype(F32)
             wave = pair if h == 0 else (nwave - 1.0) - pair
             wave = jnp.broadcast_to(wave, (step_rows, 128))
-            c, s = turns(wave * lane, float(nlon))
-            c, s = c * scale, s * scale
-            rc, rs = turns(wave * 128.0, float(nlon))
-            for t in range(nlon // 128):
+
+            def put(t, c, s):
                 fine_ref[0, 2 * h, rows, t * 128 : (t + 1) * 128] = c.astype(BF16)
                 fine_ref[0, 2 * h + 1, rows, t * 128 : (t + 1) * 128] = s.astype(BF16)
-                c, s = c * rc - s * rs, s * rc + c * rs
-        return carry
-
-    lax.fori_loop(0, devices // step_rows, block, 0)
-
-
-def coarse_kernel(nwave, pair_ref, coarse_ref):
-    devices = pair_ref.shape[1]
-    nlon = coarse_ref.shape[3] * 2
-    scale = 1.0 / math.sqrt(nlon)
-    step_rows = 16
-    lane = iota((step_rows, 128), 1).astype(F32)
-    lane_i = iota((step_rows, 128), 1)
-    tail0 = ((lane_i // 32) * 160 + 128 + lane_i % 32).astype(F32)
-
-    def block(i, carry):
-        rows = pl.ds(pl.multiple_of(i * step_rows, step_rows), step_rows)
-        for h in range(2):
-            pair = pair_ref[0, rows, :].astype(F32)
-            wave = pair if h == 0 else (nwave - 1.0) - pair
-            wave = jnp.broadcast_to(wave, (step_rows, 128))
-            amp, _ = turns(wave, 2.0 * nlon)
-            amp = amp * (2.0 * scale)
-            c, s = turns(wave * (4.0 * lane + 1.0), 2.0 * nlon)
-            c, s = c * amp, s * amp
-            rc, rs = turns(wave * 640.0, 2.0 * nlon)
-            for t in range(8):
-                coarse_ref[0, 2 * h, rows, t * 128 : (t + 1) * 128] = c.astype(BF16)
-                coarse_ref[0, 2 * h + 1, rows, t * 128 : (t + 1) * 128] = s.astype(BF16)
-                c, s = c * rc - s * rs, s * rc + c * rs
-            c, s = turns(wave * (4.0 * tail0 + 1.0), 2.0 * nlon)
-            c, s = c * amp, s * amp
-            rc, rs = turns(wave * 2560.0, 2.0 * nlon)
-            for t in range(8, 10):
-                coarse_ref[0, 2 * h, rows, t * 128 : (t + 1) * 128] = c.astype(BF16)
-                coarse_ref[0, 2 * h + 1, rows, t * 128 : (t + 1) * 128] = s.astype(BF16)
-                c, s = c * rc - s * rs, s * rc + c * rs
+
+            c, s = turns(wave * lane.astype(F32), float(nlon))
+            c, s = c * scale, s * scale
+            r64 = turns(wave * 64.0, float(nlon))
+            r128 = turned(*r64, *r64)
+            r256 = turned(*r128, *r128)
+            r320 = turned(*r256, *r64)
+            r512 = turned(*r256, *r256)
+            r640 = turned(*r320, *r320)
+            low = lane < 64
+            last = turned(
+                c, s, jnp.where(low, r256[0], r512[0]), jnp.where(low, r256[1], r512[1])
+            )
+            for t in range(16, 20):
+                put(t, *last)
+                last = turned(*last, *r640)
+            for j in range(8):
+                put(2 * j, c, s)
+                put(2 * j + 1, *turned(c, s, *r128))
+                c, s = turned(c, s, *r320)
         return carry
 
     lax.fori_loop(0, devices // step_rows, block, 0)
@@ -268,105 +253,134 @@
     )(pairs)
 
 
-def fourier_kernel(piece_ref, fine_ref, out_ref, rows):
-    blocks, group, lines, width = piece_ref.shape
-    nlon = rows.shape[1]
-
-    @pl.when(pl.program_id(0) == 0)
-    def _():
-        rows[...] = jnp.zeros_like(rows)
-        for g in range(group):
-            for j in range(blocks):
-                rows[g * 128 : g * 128 + lines, j * width : (j + 1) * width] = piece_ref[j, g]
-
-    out_ref[0] = lax.dot_general(
-        fine_ref[0].reshape(out_ref.shape[1], nlon), rows[...], NT, preferred_element_type=F32
-    )
-
-
-def fourier(piece, fine):
-    group, four, devices, nlon = fine.shape
-    levels = piece.shape[1]
-    return pl.pallas_call(
-        fourier_kernel,
-        grid=(group,),
-        out_shape=jax.ShapeDtypeStruct((group, four * devices, levels * 128), F32),
-        in_specs=[
-            pl.BlockSpec(piece.shape, lambda s: (0, 0, 0, 0)),
-            pl.BlockSpec((1, four, devices, nlon), lambda s: (s, 0, 0, 0)),
-        ],
-        out_specs=pl.BlockSpec((1, four * devices, levels * 128), lambda s: (s, 0, 0)),
-        scratch_shapes=[pltpu.VMEM((levels * 128, nlon), BF16)],
-        compiler_params=pltpu.CompilerParams(vmem_limit_bytes=16 * 2**20),
-        name="fourier",
-    )(piece, fine)
-
-
-def unpack_kernel(came_ref, code_ref, out_ref, heat):
-    blocks, groups = code_ref.shape[0], code_ref.shape[1]
-    _, both, devices = came_ref.shape
+def lay_kernel(state_ref, code_ref, out_ref, codes):
+    blocks = out_ref.shape[0]
+    groups = code_ref.shape[0]
+    lines = state_ref.shape[1]
+    codes[...] = jnp.zeros_like(codes)
+    for g in range(groups):
+        code = code_ref[g, :5, :]
+        codes[5 * g : 5 * g + 5, :] = (code // 128).astype(F32)
+        codes[5 * (groups + g) : 5 * (groups + g) + 5, :] = (code % 128).astype(F32)
+    packed = codes[...].astype(BF16)
+    for b in range(blocks):
+        for level in range(2):
+            here = state_ref[2 * b + level].astype(BF16)
+            for t in range(2):
+                first = (2 * t + level) * lines
+                out_ref[b, first : first + lines, :] = here[:, t * 128 : (t + 1) * 128]
+            out_ref[b, 4 * lines : 5 * lines, level * 64 : (level + 1) * 64] = here[:, 256:320]
+        out_ref[b, 5 * lines :, :] = packed
+
+
+def lay(state, code, blocks):
+    lines = state.shape[1]
+    return pl.pallas_call(
+        lay_kernel,
+        out_shape=jax.ShapeDtypeStruct((blocks, 5 * lines + 104, 128), BF16),
+        scratch_shapes=[pltpu.VMEM((104, 128), F32)],
+        compiler_params=pltpu.CompilerParams(vmem_limit_bytes=12 * 2**20),
+        cost_estimate=pl.CostEstimate(flops=10**6, bytes_accessed=4 * 10**6, transcendentals=0),
+        name="lay",
+    )(state, code)
+
+
+def unpack_kernel(came_ref, moved_ref, out_ref, heat):
+    blocks, both, devices = came_ref.shape
     levels = 2
+    groups = 10
     cap = both // levels
     lines = heat.shape[1] // levels
-    for j in range(blocks):
-
-        def pick(g, carry):
-            code = code_ref[j, g]
-            owner = code // 128
-            rank = code % 128
-            marks = [
-                (iota((devices, 128), 0) == owner[q : q + 1, :]).astype(F32).astype(BF16)
-                for q in range(5)
-            ]
-            found = mm(came_ref[j], jnp.concatenate(marks, axis=1))
+    first = 400
+    own = iota((devices, 128), 0).astype(F32)
+    place = iota((cap, 128), 0).astype(F32)
+
+    def block(j, carry):
+        table = came_ref[j]
+        for g in range(groups):
+            marks, ranks = [], []
             for q in range(5):
-                here = iota((cap, 128), 0) == rank[q : q + 1, :]
+                row = first + 5 * g + q
+                owner = moved_ref[j, row : row + 1, :].astype(F32)
+                row += 5 * groups
+                ranks.append(moved_ref[j, row : row + 1, :].astype(F32))
+                marks.append((own == owner).astype(F32).astype(BF16))
+            found = mm(table, jnp.concatenate(marks, axis=1))
+            for q in range(5):
+                here = place == ranks[q]
                 for level in range(levels):
                     part = found[level * cap : (level + 1) * cap, q * 128 : (q + 1) * 128]
                     value = jnp.sum(jnp.where(here, part, 0.0), axis=0, keepdims=True)
+                    line = level * lines + 4 * g
                     if q < 4:
-                        heat[j, pl.ds(level * lines + 4 * g + q, 1), :] = value
+                        heat[j, line + q : line + q + 1, :] = value
                     else:
                         tile = blocks + j // 4
                         mine = iota((1, 128), 1) // 32 == j % 4
                         for i in range(4):
-                            moved = pltpu.roll(value, (32 * (j % 4 - i)) % 128, 1)
-                            at = pl.ds(level * lines + 4 * g + i, 1)
-                            heat[tile, at, :] = jnp.where(mine, moved, heat[tile, at, :])
-            return carry
-
-        lax.fori_loop(0, groups, pick, 0, unroll=2)
+                            moved = pltpu.roll(value, (32 * (j % 4 - i) + 128) % 128, 1)
+                            old = heat[tile, line + i : line + i + 1, :]
+                            heat[tile, line + i : line + i + 1, :] = jnp.where(mine, moved, old)
+        return carry
+
+    lax.fori_loop(0, blocks, block, 0)
     for t in range(heat.shape[0]):
         out_ref[:, t * 128 : (t + 1) * 128] = heat[t].astype(BF16)
 
 
-def unpack(came, code):
-    blocks, groups = code.shape[0], code.shape[1]
-    shape = (2 * groups * 4, blocks * 160)
+def unpack(came, moved):
+    blocks = came.shape[0]
+    shape = (80, blocks * 160)
     return pl.pallas_call(
         unpack_kernel,
         out_shape=jax.ShapeDtypeStruct(shape, BF16),
         scratch_shapes=[pltpu.VMEM((shape[1] // 128, shape[0], 128), F32)],
         compiler_params=pltpu.CompilerParams(vmem_limit_bytes=12 * 2**20),
         name="unpack",
-    )(came, code)
-
-
-def heated_kernel(nwave, heat_ref, coarse_ref, base_ref, pair_ref, sites_ref, out_ref, rows, mixed):
+    )(came, moved)
+
+
+def forward_kernel(nwave, heat_ref, moved_ref, fine_ref, pair_ref, sites_ref, out_ref, rows, mixed):
     step = pl.program_id(0)
     devices = pair_ref.shape[1]
-    lines = heat_ref.shape[0] // 2
-    cap = 80
+    lines = heat_ref.shape[0]
+    cap = lines
 
     @pl.when(step == 0)
     def _():
-        twice = iota((256, 2 * lines), 0)
-        source = (twice // 128) * lines + (twice % 128) // 2
-        keep = (source == iota((256, 2 * lines), 1)) & (twice % 128 < 2 * lines)
-        rows[...] = mm(keep.astype(F32).astype(BF16), heat_ref[...]).astype(BF16)
-
-    product = base_ref[0] + lax.dot_general(
-        coarse_ref[0].reshape(4 * devices, rows.shape[1]),
+        rows[...] = jnp.zeros_like(rows)
+        place = iota((256, lines), 0)
+        source = (place // 128) * (lines // 2) + (place % 128) // 2
+        twice = (source == iota((256, lines), 1)) & (place % 128 < lines)
+        double = mm(twice.astype(F32).astype(BF16), heat_ref[...]).astype(BF16)
+        wide = (iota((128, 256), 1) // 2 == iota((128, 256), 0)).astype(F32).astype(BF16)
+        for t in range(10):
+            warm = mm(double[:, t * 128 : (t + 1) * 128], wide)
+            for level in range(2):
+                here = warm[level * 128 : level * 128 + lines, :]
+                at = slice(level * 128, level * 128 + lines)
+                if t < 8:
+                    for h in range(2):
+                        first = (2 * h + level) * lines
+                        cold = moved_ref[t, first : first + lines, :].astype(F32)
+                        span = slice(t * 256 + h * 128, t * 256 + (h + 1) * 128)
+                        rows[at, span] = (cold + here[:, h * 128 : (h + 1) * 128]).astype(BF16)
+                else:
+                    cold = jnp.concatenate(
+                        [
+                            moved_ref[
+                                4 * (t - 8) + q,
+                                4 * lines : 5 * lines,
+                                level * 64 : (level + 1) * 64,
+                            ].astype(F32)
+                            for q in range(4)
+                        ],
+                        axis=1,
+                    )
+                    rows[at, t * 256 : (t + 1) * 256] = (cold + here).astype(BF16)
+
+    product = lax.dot_general(
+        fine_ref[0].reshape(4 * devices, rows.shape[1]),
         rows[...],
         NT,
         preferred_element_type=F32,
@@ -390,27 +404,27 @@
             )
 
 
-def heated(heat, coarse, base, pairs, sites, nwave):
-    group, four, devices, half = coarse.shape
-    return pl.pallas_call(
-        functools.partial(heated_kernel, nwave),
+def forward(heat, moved, fine, pairs, sites, nwave):
+    group, four, devices, nlon = fine.shape
+    return pl.pallas_call(
+        functools.partial(forward_kernel, nwave),
         grid=(group,),
         out_shape=jax.ShapeDtypeStruct((devices, 8, group * 80), BF16),
         in_specs=[
             pl.BlockSpec(heat.shape, lambda s: (0, 0)),
-            pl.BlockSpec((1, four, devices, half), lambda s: (s, 0, 0, 0)),
-            pl.BlockSpec((1, four * devices, base.shape[2]), lambda s: (s, 0, 0)),
+            pl.BlockSpec(moved.shape, lambda s: (0, 0, 0)),
+            pl.BlockSpec((1, four, devices, nlon), lambda s: (s, 0, 0, 0)),
             pl.BlockSpec((1, devices, 1), lambda s: (s, 0, 0)),
             pl.BlockSpec(sites.shape, lambda s: (0, 0)),
         ],
         out_specs=pl.BlockSpec((devices, 8, group * 80), lambda s: (0, 0, 0)),
         scratch_shapes=[
-            pltpu.VMEM((256, half), BF16),
+            pltpu.VMEM((256, nlon), BF16),
             pltpu.VMEM((devices * 8, 128), F32),
         ],
-        compiler_params=pltpu.CompilerParams(vmem_limit_bytes=16 * 2**20),
-        name="heated",
-    )(heat, coarse, base, pairs, sites)
+        compiler_params=pltpu.CompilerParams(vmem_limit_bytes=20 * 2**20),
+        name="forward",
+    )(heat, moved, fine, pairs, sites)
 
 
 def legendre_kernel(nwave, pair_ref, came_ref, basis_ref, out_ref, right):
@@ -467,7 +481,7 @@
 def inverse_kernel(came_ref, fine_ref, out_ref, mixed, left, total):
     step = pl.program_id(0)
     devices = came_ref.shape[0]
-    blocks, _, width = out_ref.shape
+    blocks, _, _ = out_ref.shape
     for k in range(5):
 
         @pl.when(step == k)
@@ -495,7 +509,9 @@
     @pl.when(step == pl.num_programs(0) - 1)
     def _():
         for j in range(blocks):
-            out_ref[j] = total[:, j * width : (j + 1) * width].astype(BF16)
+            out_ref[j, :, :256] = total[:, j * 256 : (j + 1) * 256].astype(BF16)
+            first = blocks * 256 + j * 64
+            out_ref[j, :, 256:] = total[:, first : first + 64].astype(BF16)
 
 
 def inverse(came, fine, blocks):
@@ -543,20 +559,17 @@
     limits = jnp.concatenate([limits, limits])[None, :]
     owner = jnp.pad(holder.reshape(rows, cols), ((0, 0), (0, 256 - cols)), constant_values=-1)
 
-    piece = swap(state.astype(BF16), "lon").reshape(lon_size, level_group, lines, width)
-
     sorted_cols, code = pack(state, owner)
     outgoing = sorted_cols.reshape(5, devices, levels, 16).transpose(1, 2, 0, 3)
     came = swap(outgoing.reshape(devices, levels, 80), ALL)
-    codes = swap(jnp.broadcast_to(code[None], (lon_size,) + code.shape), "lon")
     fine = table(fine_kernel, slots, nwave, nlon)
+    laid = lay(state, code, lon_size)
+    moved = swap(laid, "lon")
     heat = radiate(came, in_hbm(depths[0]), lat_size, lon_size)
     returned = swap(heat, ALL)
-    coarse = table(coarse_kernel, slots, nwave, nlon // 2)
-    base = fourier(piece, in_hbm(fine))
     returned = returned.reshape(devices, level_group, lon_size, 80).transpose(2, 1, 3, 0)
-    warm = unpack(returned.reshape(lon_size, level_group * 80, devices), codes)
-    sending = heated(warm, in_hbm(coarse), base, slots, limits, nwave)
+    warm = unpack(returned.reshape(lon_size, level_group * 80, devices), moved)
+    sending = forward(warm, moved, in_hbm(fine), slots, limits, nwave)
     arrived = swap(sending, ALL)
     mine = lax.dynamic_slice_in_dim(pairs, me * group, group)
     spread = legendre(mine, arrived, in_hbm(basis.transpose(0, 2, 1)), nwave)

time: 219 us -> 191 us (0.87)
  Pallas kernels: 92.1 us -> 71.2 us
  starting transfers between devices: 19.5 us -> 13.7 us
  waiting for transfers between devices: 29.3 us -> 32 us
  local copies, waits for them, and re-layouts: 7.1 us -> 4.67 us
    pallas_call x2 -> x1, Pallas kernels: 19.7 us -> 10.4 us  [table(): pl.pallas_call(functools.partial(kernel, nwave), grid=(group,), out_shape...]
    pallas_call x1, Pallas kernels: 13.7 us -> 6.43 us  [unpack(): pl.pallas_call(unpack_kernel, out_shape=jax.ShapeDtypeStruct(shape, BF16)...]
    all_to_all x4 -> x3, starting transfers between devices: 19.5 us -> 13.7 us  [swap(): return lax.all_to_all(x, axes, split_axis=0, concat_axis=0, tiled=True)]
    pallas_call x2, Pallas kernels: 15.6 us -> 11.2 us  [the longest x1 10.1 us: forward(): pl.pallas_call(functools.partial(forward_kernel, nwave), grid=(group,), o...]
    all_to_all x4 -> x3, waiting for transfers between devices: 29.3 us -> 32 us  [swap(): return lax.all_to_all(x, axes, split_axis=0, concat_axis=0, tiled=True)]
  transfers between devices with their start and end apart: 4 -> 3, of which waited for: 2 -> 3; matrix products, arithmetic and copies ran while one was open for 1% -> 1% of each run, Pallas kernels for 21% -> 6%
where the time goes in v1:
time: 191 us; the launch traced here: 190 us
  Pallas kernels  71.2 us (37%)
  blocking collectives  66.2 us (35%)
  waiting for transfers between devices  32 us (17%)
  starting transfers between devices  13.7 us (7%)
  local copies, waits for them, and re-layouts  4.67 us (2%)
  other arithmetic  2.21 us (1%)
    all_to_all x3, blocking collectives, swap(): return lax.all_to_all(x, axes, split_axis=0, concat_axis=0, tiled=True)  66.2 us
    all_to_all x3, waiting for transfers between devices, swap(): return lax.all_to_all(x, axes, split_axis=0, concat_axis=0, tiled=True)  32 us
    pallas_call x1, Pallas kernels, legendre(): pl.pallas_call(functools.partial(legendre_kernel, nwave), grid_spec=pltpu...  13.7 us
    all_to_all x3, starting transfers between devices, swap(): return lax.all_to_all(x, axes, split_axis=0, concat_axis=0, tiled=True)  13.7 us
    pallas_call x1, Pallas kernels, radiate(): pl.pallas_call(radiate_kernel, grid=(lat_size,), out_shape=jax.ShapeDtype...  13 us
    pallas_call x1, Pallas kernels, table(): pl.pallas_call(functools.partial(kernel, nwave), grid=(group,), out_shape...  10.4 us
    pallas_call x1, Pallas kernels, forward(): pl.pallas_call(functools.partial(forward_kernel, nwave), grid=(group,), o...  10.1 us
    pallas_call x1, Pallas kernels, inverse(): pl.pallas_call(inverse_kernel, grid=(group,), out_shape=jax.ShapeDtypeStr...  8.27 us
  transfers between devices with their start and end apart: 3, of which 3 were waited for; matrix products, arithmetic and copies ran while one was open for 1% of the time, Pallas kernels for 6%

profile of v1, /device:TPU:1, one launch (start us, length us, event | category | flops | bytes accessed | tf_op | source)
XLA Modules:
  0.0 190.1 jit_solution(14768681770862104632)
XLA Ops:
  0.0 0.8 reduce
  0.8 0.1 reshape.21
  0.9 0.0 copy-start
  0.9 1.5 copy-done
  2.5 8.1 %pack.1 = (bf16[640,256]{1,0:T(8,128)(2,1)S(1)}, s32[10,8,128]{2,1,0:T(8,128)S(1)}) custom-call(f32[16,80,320]{2,1,0:T(8,128)S(1)} %copy-done, s32[40,256]{1,0:T(8,128)S(1)} %pad.8.owner_ref), custom_call_target="tpu_custom_call" | custom-call | flops 6000000000 | bytes 2000000 | tf_op jit(solution)/shard_map/pack/pallas_call | solution.py:110
  10.6 0.2 copy.9
  10.8 0.0 copy-start.1
  10.8 0.4 reshape.22
  11.2 0.4 copy.11
  11.7 24.8 %all_to_all.30.came_ref = bf16[128,16,80]{2,1,0:T(8,128)(2,1)S(1)} all-to-all(bf16[128,16,80]{2,1,0:T(8,128)(2,1)S(1)} %copy.11), channel_id=1, replica_groups=mesh['lat'=16,'lon'=8] {'lat','lon'}, dimensions={0} | all-to-all | bytes 655360 | tf_op jit(solution)/shard_map/all_to_all | solution.py:543
  36.5 13.0 %radiate.1 = bf16[128,2,640]{2,1,0:T(2,128)(2,1)} custom-call(bf16[128,16,80]{2,1,0:T(8,128)(2,1)S(1)} %all_to_all.30.came_ref, bf16[16,16,10240]{2,1,0:T(8,128)(2,1)} %bitcast.19), custom_call_target="tpu_custom_call" | custom-call | tf_op jit(solution)/shard_map/radiate/pallas_call | solution.py:161
  49.6 4.6 %all-to-all-start.1 = ((bf16[128,2,640]{2,1,0:T(2,128)(2,1)}), bf16[128,2,640]{2,1,0:T(2,128)(2,1)S(1)}, u32[]{:S(2)}, u32[]{:S(2)}) async-start(bf16[128,2,640]{2,1,0:T(2,128)(2,1)} %radiate.1), calls=%async_computation.1 | async-start | bytes 655360 | tf_op jit(solution)/shard_map/all_to_all | solution.py:543
  54.2 0.0 copy-done.1
  54.2 1.1 lay.1
  55.3 10.5 %all-to-all-done.1 = bf16[128,2,640]{2,1,0:T(2,128)(2,1)S(1)} async-done(((bf16[128,2,640]{2,1,0:T(2,128)(2,1)}), bf16[128,2,640]{2,1,0:T(2,128)(2,1)S(1)}, u32[]{:S(2)}, u32[]{:S(2)}) %all-to-all-start.1) | async-done | bytes 327712 | tf_op jit(solution)/shard_map/all_to_all | solution.py:543
  65.8 4.7 %all-to-all-start.2 = ((bf16[8,504,128]{2,1,0:T(8,128)(2,1)}), bf16[8,504,128]{2,1,0:T(8,128)(2,1)S(1)}, u32[]{:S(2)}, u32[]{:S(2)}) async-start(bf16[8,504,128]{2,1,0:T(8,128)(2,1)} %lay.1), calls=%async_computation.2 | async-start | bytes 2064384 | tf_op jit(solution)/shard_map/all_to_all | solution.py:543
  70.4 0.0 copy-done.3
  70.5 0.2 reshape.26
  70.7 1.0 copy.15.pair_ref
  71.7 10.4 %shard_map.64.fine_ref = bf16[5,4,128,2560]{3,2,1,0:T(8,128)(2,1)} custom-call(s32[5,128,1]{2,1,0:T(8,128)S(1)} %copy.15.pair_ref), custom_call_target="tpu_custom_call" | custom-call | flops 65536000 | bytes 13107200 | tf_op jit(solution)/shard_map/pallas_call | solution.py:245
  82.2 0.6 copy.12
  82.8 2.4 %all-to-all-done.2.moved_ref = bf16[8,504,128]{2,1,0:T(8,128)(2,1)S(1)} async-done(((bf16[8,504,128]{2,1,0:T(8,128)(2,1)}), bf16[8,504,128]{2,1,0:T(8,128)(2,1)S(1)}, u32[]{:S(2)}, u32[]{:S(2)}) %all-to-all-start.2) | async-done | bytes 1032224 | tf_op jit(solution)/shard_map/all_to_all | solution.py:543
  85.3 6.4 %unpack.1.heat_ref = bf16[80,1280]{1,0:T(8,128)(2,1)S(1)} custom-call(bf16[8,160,128]{2,1,0:T(8,128)(2,1)S(1)} %bitcast.16, bf16[8,504,128]{2,1,0:T(8,128)(2,1)S(1)} %all-to-all-done.2.moved_ref), custom_call_target="tpu_custom_call" | custom-call | tf_op jit(solution)/shard_map/unpack/pallas_call | solution.py:334
  91.7 10.1 %forward.1 = bf16[128,8,400]{2,1,0:T(8,128)(2,1)} custom-call(bf16[80,1280]{1,0:T(8,128)(2,1)S(1)} %unpack.1.heat_ref, bf16[8,504,128]{2,1,0:T(8,128)(2,1)S(1)} %all-to-all-done.2.moved_ref, bf16[5,4,128,2560]{3,2,1,0:T(8,128)(2,1)} %shard_map.64.fine_ref, s32[5,128,1]{2,1,0:T(8,128)S(1)} %copy.15.pair_ref, s32[1,256]{1,0:T(1,128)S(1)} %bitcast.17), custom_call_target="tpu_custom_call" | custom-call | tf_op jit(solution)/shard_map/forward/pallas_call | solution.py:409
  101.8 4.4 %all-to-all-start.3 = ((bf16[128,8,400]{2,1,0:T(8,128)(2,1)}), bf16[128,8,400]{2,1,0:T(8,128)(2,1)S(1)}, u32[]{:S(2)}, u32[]{:S(2)}) async-start(bf16[128,8,400]{2,1,0:T(8,128)(2,1)} %forward.1), calls=%async_computation.3 | async-start | bytes 2097152 | tf_op jit(solution)/shard_map/all_to_all | solution.py:543
  106.2 0.1 dynamic_slice.3.pair_ref
  106.3 19.1 %all-to-all-done.3.came_ref = bf16[128,8,400]{2,1,0:T(8,128)(2,1)S(1)} async-done(((bf16[128,8,400]{2,1,0:T(8,128)(2,1)}), bf16[128,8,400]{2,1,0:T(8,128)(2,1)S(1)}, u32[]{:S(2)}, u32[]{:S(2)}) %all-to-all-start.3) | async-done | bytes 819232 | tf_op jit(solution)/shard_map/all_to_all | solution.py:543
  125.4 13.7 %legendre.1 = bf16[128,8,400]{2,1,0:T(8,128)(2,1)S(1)} custom-call(s32[5]{0:T(128)S(1)} %dynamic_slice.3.pair_ref, bf16[128,8,400]{2,1,0:T(8,128)(2,1)S(1)} %all-to-all-done.3.came_ref, bf16[5,1344,1280]{2,1,0:T(8,128)(2,1)} %bitcast.18), custom_call_target="tpu_custom_call" | custom-call | tf_op jit(solution)/shard_map/legendre/pallas_call | solution.py:463
  139.1 23.4 %all_to_all.31.came_ref = bf16[128,8,400]{2,1,0:T(8,128)(2,1)S(1)} all-to-all(bf16[128,8,400]{2,1,0:T(8,128)(2,1)S(1)} %legendre.1), channel_id=1, replica_groups=mesh['lat'=16,'lon'=8] {'lat','lon'}, dimensions={0} | all-to-all | bytes 1638400 | tf_op jit(solution)/shard_map/all_to_all | solution.py:543
  162.4 8.3 %inverse.1 = bf16[8,160,320]{2,1,0:T(8,128)(2,1)S(1)} custom-call(bf16[128,8,400]{2,1,0:T(8,128)(2,1)S(1)} %all_to_all.31.came_ref, bf16[5,4,128,2560]{3,2,1,0:T(8,128)(2,1)} %shard_map.64.fine_ref), custom_call_target="tpu_custom_call" | custom-call | tf_op jit(solution)/shard_map/inverse/pallas_call | solution.py:519
  170.7 18.0 %all_to_all.32 = bf16[8,160,320]{2,1,0:T(8,128)(2,1)S(1)} all-to-all(bf16[8,160,320]{2,1,0:T(8,128)(2,1)S(1)} %inverse.1), channel_id=1, replica_groups=mesh['lat'=16,'lon'=8] {'lon'}, dimensions={0} | all-to-all | bytes 1638400 | tf_op jit(solution)/shard_map/all_to_all | solution.py:543
  188.7 1.4 convert.1
  (8 shorter events, 0.1 us)
Async XLA Ops:
  0.9 1.5 copy-start
  10.8 43.4 %copy-start.1 = (f32[16,80,320]{2,1,0:T(8,128)S(1)}, f32[16,80,320]{2,1,0:T(8,128)}, u32[]{:S(2)}) copy-start(f32[16,80,320]{2,1,0:T(8,128)} %state_ref.3) | copy-start | bytes 4915204
  36.5 33.9 %copy-start.3 = (s32[80]{0:T(128)S(1)}, s32[80]{0:T(128)}, u32[]{:S(2)}) copy-start(s32[80]{0:T(128)} %param.10) | copy-start | bytes 964
  36.5 33.9 %copy-start.2 = (s32[640]{0:T(1024)S(1)}, s32[640]{0:T(1024)}, u32[]{:S(2)}) copy-start(s32[640]{0:T(1024)} %param.9) | copy-start | bytes 7684
  49.6 16.2 %all-to-all-start.1 = ((bf16[128,2,640]{2,1,0:T(2,128)(2,1)}), bf16[128,2,640]{2,1,0:T(2,128)(2,1)S(1)}, u32[]{:S(2)}, u32[]{:S(2)}) async-start(bf16[128,2,640]{2,1,0:T(2,128)(2,1)} %radiate.1), calls=%async_computation.1 | async-start | bytes 655360 | tf_op jit(solution)/shard_map/all_to_all | solution.py:543
  65.8 19.5 %all-to-all-start.2 = ((bf16[8,504,128]{2,1,0:T(8,128)(2,1)}), bf16[8,504,128]{2,1,0:T(8,128)(2,1)S(1)}, u32[]{:S(2)}, u32[]{:S(2)}) async-start(bf16[8,504,128]{2,1,0:T(8,128)(2,1)} %lay.1), calls=%async_computation.2 | async-start | bytes 2064384 | tf_op jit(solution)/shard_map/all_to_all | solution.py:543
  101.8 23.6 %all-to-all-start.3 = ((bf16[128,8,400]{2,1,0:T(8,128)(2,1)}), bf16[128,8,400]{2,1,0:T(8,128)(2,1)S(1)}, u32[]{:S(2)}, u32[]{:S(2)}) async-start(bf16[128,8,400]{2,1,0:T(8,128)(2,1)} %forward.1), calls=%async_computation.3 | async-start | bytes 2097152 | tf_op jit(solution)/shard_map/all_to_all | solution.py:543

commit v2 on v1

--- a/solution.py
+++ b/solution.py
@@ -31,22 +31,17 @@
     return mm(hi, b) + mm(lo, b)
 
 
-def pack_kernel(state_ref, owner_ref, out_ref, code_ref, halves, coarse, marks, owners, values, total):
+def pack_kernel(
+    state_ref, owner_ref, out_ref, code_ref, state, halves, coarse, marks, owners, values, total, sem
+):
     levels, lines, width = state_ref.shape
     rows, lanes = owner_ref.shape
     devices = 128
     low = 16
     high = out_ref.shape[0] // devices
+    fetch = pltpu.make_async_copy(state_ref, state, sem)
+    fetch.start()
     pool_x = (iota((width, lanes), 0) // 2 == iota((width, lanes), 1)).astype(F32).astype(BF16)
-    summed = split_mm_right(state_ref[...].reshape(levels * lines, width), pool_x)
-    for t in range(2):
-        halves[t] = summed[:, t * 128 : (t + 1) * 128]
-    for level in range(levels):
-        for t in range(2):
-            even = halves[t, pl.ds(level * lines, rows, stride=2), :]
-            odd = halves[t, pl.ds(level * lines + 1, rows, stride=2), :]
-            mean = 0.25 * (even + odd)
-            coarse[level, :, t * 128 : (t + 1) * 128] = mean.astype(BF16).astype(F32)
     before = (iota((lanes, lanes), 0) < iota((lanes, lanes), 1)).astype(F32).astype(BF16)
     total[...] = jnp.zeros_like(total)
     short = iota((8, 128), 1) < 32
@@ -77,15 +72,23 @@
             code_ref[2 * c + i] = jnp.concatenate(
                 [code[4 * i : 4 * i + 4, :128], ends[i], jnp.zeros((3, 128), I32)], axis=0
             )
-        lines8 = [code[u : u + 1, :128] for u in range(8)] + ends
+        return base
+
+    def sort(c, carry):
+        start = pl.multiple_of(c * 8, 8)
+        codes = [code_ref[2 * c + i] for i in range(2)]
         temps = []
         for level in range(levels):
             block = coarse[level, pl.ds(start, 8), :]
-            temps.append([block[u : u + 1, :128] for u in range(8)] + tails(block[:, 128:]))
+            ends = tails(block[:, 128:])
+            temps.append(
+                [block[4 * i + u : 4 * i + u + 1, :128] if u < 4 else ends[i] for i in range(2) for u in range(5)]
+            )
         for u in range(10):
             span = slice(u * 128, (u + 1) * 128)
-            owner = lines8[u] // 128
-            rank = lines8[u] % 128
+            code = codes[u // 5][u % 5 : u % 5 + 1, :]
+            owner = code // 128
+            rank = code % 128
             match = (iota((devices, 128), 0) == owner).astype(F32)
             for h in range(high):
                 part = ((rank // low) == h).astype(F32)
@@ -98,9 +101,20 @@
         total[...] += lax.dot_general(
             owners[...], values[...], NT, preferred_element_type=F32
         )
-        return base
+        return carry
 
     lax.fori_loop(0, rows // 8, chunk, jnp.zeros((devices, devices), F32))
+    fetch.wait()
+    summed = split_mm_right(state[...].reshape(levels * lines, width), pool_x)
+    for t in range(2):
+        halves[t] = summed[:, t * 128 : (t + 1) * 128]
+    for level in range(levels):
+        for t in range(2):
+            even = halves[t, pl.ds(level * lines, rows, stride=2), :]
+            odd = halves[t, pl.ds(level * lines + 1, rows, stride=2), :]
+            mean = 0.25 * (even + odd)
+            coarse[level, :, t * 128 : (t + 1) * 128] = mean.astype(BF16).astype(F32)
+    lax.fori_loop(0, rows // 8, sort, 0)
     out_ref[...] = total[...].astype(BF16)
 
 
@@ -113,13 +127,19 @@
             jax.ShapeDtypeStruct((640, levels * 16), BF16),
             jax.ShapeDtypeStruct((rows // 4, 8, 128), I32),
         ),
+        in_specs=[
+            pl.BlockSpec(memory_space=pltpu.HBM),
+            pl.BlockSpec(memory_space=pltpu.VMEM),
+        ],
         scratch_shapes=[
+            pltpu.VMEM(state.shape, F32),
             pltpu.VMEM((2, levels * lines, 128), F32),
             pltpu.VMEM((levels, rows, lanes), F32),
             pltpu.VMEM((8 * 128, lanes), BF16),
             pltpu.VMEM((640, 1280), BF16),
             pltpu.VMEM((levels * 16, 1280), BF16),
             pltpu.VMEM((640, levels * 16), F32),
+            pltpu.SemaphoreType.DMA,
         ],
         compiler_params=pltpu.CompilerParams(vmem_limit_bytes=20 * 2**20),
         cost_estimate=pl.CostEstimate(flops=6 * 10**9, bytes_accessed=2 * 10**6, transcendentals=0),
@@ -199,16 +219,16 @@
 
 def fine_kernel(nwave, pair_ref, fine_ref):
     devices = pair_ref.shape[1]
-    nlon = fine_ref.shape[3]
+    nlon = fine_ref.shape[3] * 2
     scale = 1.0 / math.sqrt(nlon)
-    step_rows = 16
+    step_rows = 32
     lane = iota((step_rows, 128), 1)
 
     def block(i, carry):
         rows = pl.ds(pl.multiple_of(i * step_rows, step_rows), step_rows)
         for h in range(2):
-            pair = pair_ref[0, rows, :].astype(F32)
-            wave = pair if h == 0 else (nwave - 1.0) - pair
+            pair = pair_ref[0, rows, :]
+            wave = jnp.where(pair % 2 == h, pair, nwave - 1 - pair).astype(F32)
             wave = jnp.broadcast_to(wave, (step_rows, 128))
 
             def put(t, c, s):
@@ -227,10 +247,10 @@
             last = turned(
                 c, s, jnp.where(low, r256[0], r512[0]), jnp.where(low, r256[1], r512[1])
             )
-            for t in range(16, 20):
+            for t in range(8, 10):
                 put(t, *last)
                 last = turned(*last, *r640)
-            for j in range(8):
+            for j in range(4):
                 put(2 * j, c, s)
                 put(2 * j + 1, *turned(c, s, *r128))
                 c, s = turned(c, s, *r320)
@@ -354,43 +374,42 @@
         twice = (source == iota((256, lines), 1)) & (place % 128 < lines)
         double = mm(twice.astype(F32).astype(BF16), heat_ref[...]).astype(BF16)
         wide = (iota((128, 256), 1) // 2 == iota((128, 256), 0)).astype(F32).astype(BF16)
-        for t in range(10):
-            warm = mm(double[:, t * 128 : (t + 1) * 128], wide)
+        for t in range(5):
+            near, far = (t, t + 4) if t < 4 else (8, 9)
+            warm = [mm(double[:, m * 128 : (m + 1) * 128], wide) for m in (near, far)]
             for level in range(2):
-                here = warm[level * 128 : level * 128 + lines, :]
                 at = slice(level * 128, level * 128 + lines)
-                if t < 8:
-                    for h in range(2):
-                        first = (2 * h + level) * lines
-                        cold = moved_ref[t, first : first + lines, :].astype(F32)
-                        span = slice(t * 256 + h * 128, t * 256 + (h + 1) * 128)
-                        rows[at, span] = (cold + here[:, h * 128 : (h + 1) * 128]).astype(BF16)
-                else:
-                    cold = jnp.concatenate(
-                        [
-                            moved_ref[
-                                4 * (t - 8) + q,
-                                4 * lines : 5 * lines,
-                                level * 64 : (level + 1) * 64,
-                            ].astype(F32)
+                hot = []
+                for m, up in zip((near, far), warm):
+                    if m < 8:
+                        first = [(2 * h + level) * lines for h in range(2)]
+                        cold = [moved_ref[m, f : f + lines, :] for f in first]
+                    else:
+                        side = slice(level * 64, (level + 1) * 64)
+                        cold = [
+                            moved_ref[4 * (m - 8) + q, 4 * lines : 5 * lines, side]
                             for q in range(4)
-                        ],
-                        axis=1,
-                    )
-                    rows[at, t * 256 : (t + 1) * 256] = (cold + here).astype(BF16)
-
-    product = lax.dot_general(
-        fine_ref[0].reshape(4 * devices, rows.shape[1]),
-        rows[...],
-        NT,
-        preferred_element_type=F32,
-    )
+                        ]
+                    cold = jnp.concatenate([c.astype(F32) for c in cold], axis=1)
+                    hot.append(cold + up[at, :])
+                span = slice(t * 256, (t + 1) * 256)
+                rows[0, at, span] = (hot[0] + hot[1]).astype(BF16)
+                rows[1, at, span] = (hot[0] - hot[1]).astype(BF16)
+
+    products = [
+        lax.dot_general(
+            fine_ref[0, 2 * e : 2 * e + 2].reshape(2 * devices, rows.shape[2]),
+            rows[e],
+            NT,
+            preferred_element_type=F32,
+        )
+        for e in range(2)
+    ]
     pair = pair_ref[0]
     for k in range(4):
-        wave = pair if k < 2 else nwave - 1 - pair
-        part = jnp.where(
-            2 * wave < sites_ref[...], product[k * devices : (k + 1) * devices, :], 0.0
-        )
+        wave = jnp.where(pair % 2 == k // 2, pair, nwave - 1 - pair)
+        product = products[k // 2][(k % 2) * devices : (k % 2 + 1) * devices, :]
+        part = jnp.where(2 * wave < sites_ref[...], product, 0.0)
         for level in range(2):
             mixed[pl.ds(level * 4 + k, devices, stride=8), :] = part[
                 :, level * 128 : (level + 1) * 128
@@ -419,7 +438,7 @@
         ],
         out_specs=pl.BlockSpec((devices, 8, group * 80), lambda s: (0, 0, 0)),
         scratch_shapes=[
-            pltpu.VMEM((256, nlon), BF16),
+            pltpu.VMEM((2, 256, nlon), BF16),
             pltpu.VMEM((devices * 8, 128), F32),
         ],
         compiler_params=pltpu.CompilerParams(vmem_limit_bytes=20 * 2**20),
@@ -427,53 +446,70 @@
     )(heat, moved, fine, pairs, sites)
 
 
-def legendre_kernel(nwave, pair_ref, came_ref, basis_ref, out_ref, right):
-    step = pl.program_id(0)
-    ndeg, nlat = basis_ref.shape[1], basis_ref.shape[2]
+def legendre_kernel(nwave, pair_ref, came_ref, basis_ref, out_ref, held, right, damped, sems):
+    group, ndeg, nlat = held.shape
     bands = nlat // 80
-    for k in range(5):
-
-        @pl.when(step == k)
-        def _(k=k):
-            for a in range(bands):
-                block = came_ref[a * 8 : (a + 1) * 8, :, k * 80 : (k + 1) * 80].astype(F32)
-                right[:, a * 80 : (a + 1) * 80] = block.reshape(64, 80).astype(BF16)
-
-    pair = pair_ref[step]
-    full = lax.dot_general(right[...], basis_ref[0], NT, preferred_element_type=F32)
-    coeff = iota((64, ndeg), 1)
-    head = (iota((64, ndeg), 0) % 4) < 2
-    first = coeff < nwave - pair
-    degree = jnp.where(first, pair + coeff, coeff - 1).astype(F32)
-    factor = 1.0 / (1.0 + DIFFUSION * degree * (degree + 1.0) / (nwave * nwave))
-    keep = (first & head) | (jnp.logical_not(first) & jnp.logical_not(head) & (coeff <= nwave))
-    damped = jnp.where(keep, full * factor, 0.0).astype(BF16)
-    synth = mm(damped, basis_ref[0])
-    for k in range(5):
-
-        @pl.when(step == k)
-        def _(k=k):
-            for a in range(bands):
-                block = synth[:, a * 80 : (a + 1) * 80].reshape(8, 8, 80)
-                out_ref[a * 8 : (a + 1) * 8, :, k * 80 : (k + 1) * 80] = block.astype(BF16)
+    cuts = (0, 512, 1024, ndeg)
+    spans = [pl.ds(cuts[q], cuts[q + 1] - cuts[q]) for q in range(3)]
+
+    def copy(s, q):
+        return pltpu.make_async_copy(
+            basis_ref.at[s, spans[q]], held.at[s, spans[q]], sems.at[s, q]
+        )
+
+    for s in range(group):
+        for q in range(3):
+            copy(s, q).start()
+
+    for s in range(group):
+        lanes = slice(s * 80, (s + 1) * 80)
+        for a in range(bands):
+            block = came_ref[a * 8 : (a + 1) * 8, :, lanes].astype(F32)
+            right[s, :, a * 80 : (a + 1) * 80] = block.reshape(64, 80).astype(BF16)
+    for s in range(group):
+        lanes = slice(s * 80, (s + 1) * 80)
+        pair = pair_ref[s]
+        for q in range(3):
+            copy(s, q).wait()
+            size = cuts[q + 1] - cuts[q]
+            full = lax.dot_general(
+                right[s], held[s, spans[q], :], NT, preferred_element_type=F32
+            )
+            coeff = iota((64, size), 1) + cuts[q]
+            head = (iota((64, size), 0) % 4) // 2 == pair % 2
+            first = coeff < nwave - pair
+            degree = jnp.where(first, pair + coeff, coeff - 1).astype(F32)
+            factor = 1.0 / (1.0 + DIFFUSION * degree * (degree + 1.0) / (nwave * nwave))
+            keep = (first & head) | (
+                jnp.logical_not(first) & jnp.logical_not(head) & (coeff <= nwave)
+            )
+            damped[s, :, cuts[q] : cuts[q + 1]] = jnp.where(keep, full * factor, 0.0).astype(
+                BF16
+            )
+        synth = mm(damped[s], held[s])
+        for a in range(bands):
+            block = synth[:, a * 80 : (a + 1) * 80].reshape(8, 8, 80)
+            out_ref[a * 8 : (a + 1) * 8, :, lanes] = block.astype(BF16)
 
 
 def legendre(pairs, came, basis, nwave):
     group, ndeg, nlat = basis.shape
     return pl.pallas_call(
         functools.partial(legendre_kernel, nwave),
-        grid_spec=pltpu.PrefetchScalarGridSpec(
-            num_scalar_prefetch=1,
-            grid=(group,),
-            in_specs=[
-                pl.BlockSpec(came.shape, lambda s, p: (0, 0, 0)),
-                pl.BlockSpec((1, ndeg, nlat), lambda s, p: (s, 0, 0)),
-            ],
-            out_specs=pl.BlockSpec(came.shape, lambda s, p: (0, 0, 0)),
-            scratch_shapes=[pltpu.VMEM((64, nlat), BF16)],
-        ),
+        in_specs=[
+            pl.BlockSpec(memory_space=pltpu.SMEM),
+            pl.BlockSpec(memory_space=pltpu.VMEM),
+            pl.BlockSpec(memory_space=pltpu.HBM),
+        ],
+        out_specs=pl.BlockSpec(memory_space=pltpu.VMEM),
+        scratch_shapes=[
+            pltpu.VMEM((group, ndeg, nlat), BF16),
+            pltpu.VMEM((group, 64, nlat), BF16),
+            pltpu.VMEM((group, 64, ndeg), BF16),
+            pltpu.SemaphoreType.DMA((group, 3)),
+        ],
         out_shape=jax.ShapeDtypeStruct(came.shape, BF16),
-        compiler_params=pltpu.CompilerParams(vmem_limit_bytes=24 * 2**20),
+        compiler_params=pltpu.CompilerParams(vmem_limit_bytes=32 * 2**20),
         name="legendre",
     )(pairs, came, basis)
 
@@ -481,7 +517,7 @@
 def inverse_kernel(came_ref, fine_ref, out_ref, mixed, left, total):
     step = pl.program_id(0)
     devices = came_ref.shape[0]
-    blocks, _, _ = out_ref.shape
+    blocks = out_ref.shape[0]
     for k in range(5):
 
         @pl.when(step == k)
@@ -496,43 +532,84 @@
             left[level * 80 : (level + 1) * 80, k * devices : (k + 1) * devices] = part.T[
                 :80, :
             ].astype(BF16)
-    product = mm(left[...], fine_ref[0].reshape(4 * devices, total.shape[1]))
-
-    @pl.when(step == 0)
-    def _():
-        total[...] = product
-
-    @pl.when(step > 0)
-    def _():
-        total[...] += product
+    half = fine_ref.shape[3]
+    for e in range(2):
+        product = mm(
+            left[:, 2 * e * devices : 2 * (e + 1) * devices],
+            fine_ref[0, 2 * e : 2 * e + 2].reshape(2 * devices, half),
+        )
+
+        @pl.when(step == 0)
+        def _():
+            total[e] = product
+
+        @pl.when(step > 0)
+        def _():
+            total[e] += product
 
     @pl.when(step == pl.num_programs(0) - 1)
     def _():
         for j in range(blocks):
-            out_ref[j, :, :256] = total[:, j * 256 : (j + 1) * 256].astype(BF16)
-            first = blocks * 256 + j * 64
-            out_ref[j, :, 256:] = total[:, first : first + 64].astype(BF16)
+            k = j % 4
+            for t in range(3):
+                first = k * 256 + t * 128 if t < 2 else 1024 + k * 64
+                span = slice(first, first + (128 if t < 2 else 64))
+                even, odd = total[0, :, span], total[1, :, span]
+                value = (even + odd if j < 4 else even - odd).astype(BF16)
+                if t < 2:
+                    out_ref[j, t * 160 : (t + 1) * 160, :] = value
+                else:
+                    out_ref[j, 320:, :64] = value[:80]
+                    out_ref[j, 320:, 64:] = value[80:]
 
 
 def inverse(came, fine, blocks):
-    group, four, devices, nlon = fine.shape
+    group, four, devices, half = fine.shape
     return pl.pallas_call(
         inverse_kernel,
         grid=(group,),
-        out_shape=jax.ShapeDtypeStruct((blocks, 160, nlon // blocks), BF16),
+        out_shape=jax.ShapeDtypeStruct((blocks, 400, 128), BF16),
         in_specs=[
             pl.BlockSpec(came.shape, lambda s: (0, 0, 0)),
-            pl.BlockSpec((1, four, devices, nlon), lambda s: (s, 0, 0, 0)),
-        ],
-        out_specs=pl.BlockSpec((blocks, 160, nlon // blocks), lambda s: (0, 0, 0)),
+            pl.BlockSpec((1, four, devices, half), lambda s: (s, 0, 0, 0)),
+        ],
+        out_specs=pl.BlockSpec((blocks, 400, 128), lambda s: (0, 0, 0)),
         scratch_shapes=[
             pltpu.VMEM((devices * 8, 128), F32),
             pltpu.VMEM((160, four * devices), BF16),
-            pltpu.VMEM((160, nlon), F32),
+            pltpu.VMEM((2, 160, half), F32),
         ],
         compiler_params=pltpu.CompilerParams(vmem_limit_bytes=24 * 2**20),
         name="inverse",
     )(came, fine)
+
+
+def finish_kernel(came_ref, out_ref):
+    lines = out_ref.shape[1]
+    for b in range(came_ref.shape[0]):
+        for level in range(2):
+            for t in range(2):
+                first = (2 * t + level) * lines
+                out_ref[2 * b + level, :, t * 128 : (t + 1) * 128] = came_ref[
+                    b, first : first + lines, :
+                ].astype(F32)
+            out_ref[2 * b + level, :, 256:] = came_ref[
+                b, 4 * lines :, level * 64 : (level + 1) * 64
+            ].astype(F32)
+
+
+def finish(came, levels, lines, width):
+    blocks, rows, _ = came.shape
+    steps = 2
+    return pl.pallas_call(
+        finish_kernel,
+        grid=(steps,),
+        out_shape=jax.ShapeDtypeStruct((levels, lines, width), F32),
+        in_specs=[pl.BlockSpec((blocks // steps, rows, 128), lambda s: (s, 0, 0))],
+        out_specs=pl.BlockSpec((levels // steps, lines, width), lambda s: (s, 0, 0)),
+        compiler_params=pltpu.CompilerParams(vmem_limit_bytes=12 * 2**20),
+        name="finish",
+    )(came)
 
 
 def in_hbm(x):
@@ -562,7 +639,7 @@
     sorted_cols, code = pack(state, owner)
     outgoing = sorted_cols.reshape(5, devices, levels, 16).transpose(1, 2, 0, 3)
     came = swap(outgoing.reshape(devices, levels, 80), ALL)
-    fine = table(fine_kernel, slots, nwave, nlon)
+    fine = table(fine_kernel, slots, nwave, nlon // 2)
     laid = lay(state, code, lon_size)
     moved = swap(laid, "lon")
     heat = radiate(came, in_hbm(depths[0]), lat_size, lon_size)
@@ -575,8 +652,7 @@
     spread = legendre(mine, arrived, in_hbm(basis.transpose(0, 2, 1)), nwave)
     back = swap(spread, ALL)
     grid = inverse(back, in_hbm(fine), lon_size)
-    grid = swap(grid, "lon")
-    return grid.reshape(levels, lines, width).astype(F32)
+    return finish(swap(grid, "lon"), levels, lines, width)
 
 
 def solution(mesh):

time: 191 us -> 185 us (0.969)
  Pallas kernels: 71.2 us -> 64.9 us
  waiting for transfers between devices: 32 us -> 35.5 us
    pallas_call x1, Pallas kernels: 10.4 us -> 6.91 us  [table(): pl.pallas_call(functools.partial(kernel, nwave), grid=(group,), out_shape...]
    all_to_all x3, waiting for transfers between devices: 32 us -> 35.5 us  [swap(): return lax.all_to_all(x, axes, split_axis=0, concat_axis=0, tiled=True)]
    pallas_call x1, Pallas kernels: 10.1 us -> 7.82 us  [forward(): pl.pallas_call(functools.partial(forward_kernel, nwave), grid=(group,), o...]
    pallas_call x1 -> x2, Pallas kernels: 13.7 us -> 14.5 us  [the longest x1 13.2 us: legendre(): pl.pallas_call(functools.partial(legendre_kernel, nwave), in_specs=[pl.Bl...]
  transfers between devices with their start and end apart: 3 -> 3, of which waited for: 3 -> 3; matrix products, arithmetic and copies ran while one was open for 1% -> 1% of each run, Pallas kernels for 6% -> 4%
where the time goes in v2:
time: 185 us
  Pallas kernels  64.9 us (35%)
  blocking collectives  64.8 us (35%)
  waiting for transfers between devices  35.5 us (19%)
  starting transfers between devices  13.7 us (7%)
  local copies, waits for them, and re-layouts  4.67 us (3%)
    all_to_all x3, blocking collectives, swap(): return lax.all_to_all(x, axes, split_axis=0, concat_axis=0, tiled=True)  64.8 us
    all_to_all x3, waiting for transfers between devices, swap(): return lax.all_to_all(x, axes, split_axis=0, concat_axis=0, tiled=True)  35.5 us
    all_to_all x3, starting transfers between devices, swap(): return lax.all_to_all(x, axes, split_axis=0, concat_axis=0, tiled=True)  13.7 us
    pallas_call x1, Pallas kernels, legendre(): pl.pallas_call(functools.partial(legendre_kernel, nwave), in_specs=[pl.Bl...  13.2 us
    pallas_call x1, Pallas kernels, radiate(): pl.pallas_call(radiate_kernel, grid=(lat_size,), out_shape=jax.ShapeDtype...  13 us
    pallas_call x1, Pallas kernels, pack(): pl.pallas_call(pack_kernel, out_shape=(jax.ShapeDtypeStruct((640, levels...  8.05 us
    pallas_call x1, Pallas kernels, forward(): pl.pallas_call(functools.partial(forward_kernel, nwave), grid=(group,), o...  7.82 us
    pallas_call x1, Pallas kernels, inverse(): pl.pallas_call(inverse_kernel, grid=(group,), out_shape=jax.ShapeDtypeStr...  6.95 us
  transfers between devices with their start and end apart: 3, of which 3 were waited for; matrix products, arithmetic and copies ran while one was open for 1% of the time, Pallas kernels for 4%

profile of v2, /device:TPU:1, one launch (start us, length us, event | category | flops | bytes accessed | tf_op | source)
XLA Modules:
  0.0 184.5 jit_solution(2626666774705586768)
XLA Ops:
  0.0 0.8 reduce
  0.8 0.1 reshape.18
  0.9 0.0 copy-start
  0.9 1.5 copy-done
  2.5 8.0 %pack.1 = (bf16[640,256]{1,0:T(8,128)(2,1)S(1)}, s32[10,8,128]{2,1,0:T(8,128)S(1)}) custom-call(f32[16,80,320]{2,1,0:T(8,128)S(1)} %copy-done, s32[40,256]{1,0:T(8,128)S(1)} %pad.8.owner_ref), custom_call_target="tpu_custom_call" | custom-call | flops 6000000000 | bytes 2000000 | tf_op jit(solution)/shard_map/pack/pallas_call | solution.py:124
  10.5 0.2 copy.9
  10.7 0.0 copy-start.1
  10.7 0.4 reshape.19
  11.2 0.4 copy.11
  11.6 24.8 %all_to_all.30.came_ref = bf16[128,16,80]{2,1,0:T(8,128)(2,1)S(1)} all-to-all(bf16[128,16,80]{2,1,0:T(8,128)(2,1)S(1)} %copy.11), channel_id=1, replica_groups=mesh['lat'=16,'lon'=8] {'lat','lon'}, dimensions={0} | all-to-all | bytes 655360 | tf_op jit(solution)/shard_map/all_to_all | solution.py:620
  36.5 13.0 %radiate.1 = bf16[128,2,640]{2,1,0:T(2,128)(2,1)} custom-call(bf16[128,16,80]{2,1,0:T(8,128)(2,1)S(1)} %all_to_all.30.came_ref, bf16[16,16,10240]{2,1,0:T(8,128)(2,1)} %bitcast.17), custom_call_target="tpu_custom_call" | custom-call | tf_op jit(solution)/shard_map/radiate/pallas_call | solution.py:181
  49.5 4.6 %all-to-all-start.1 = ((bf16[128,2,640]{2,1,0:T(2,128)(2,1)}), bf16[128,2,640]{2,1,0:T(2,128)(2,1)S(1)}, u32[]{:S(2)}, u32[]{:S(2)}) async-start(bf16[128,2,640]{2,1,0:T(2,128)(2,1)} %radiate.1), calls=%async_computation.1 | async-start | bytes 655360 | tf_op jit(solution)/shard_map/all_to_all | solution.py:620
  54.1 0.0 copy-done.1
  54.1 1.1 lay.1
  55.3 10.5 %all-to-all-done.1 = bf16[128,2,640]{2,1,0:T(2,128)(2,1)S(1)} async-done(((bf16[128,2,640]{2,1,0:T(2,128)(2,1)}), bf16[128,2,640]{2,1,0:T(2,128)(2,1)S(1)}, u32[]{:S(2)}, u32[]{:S(2)}) %all-to-all-start.1) | async-done | bytes 327712 | tf_op jit(solution)/shard_map/all_to_all | solution.py:620
  65.7 4.7 %all-to-all-start.2 = ((bf16[8,504,128]{2,1,0:T(8,128)(2,1)}), bf16[8,504,128]{2,1,0:T(8,128)(2,1)S(1)}, u32[]{:S(2)}, u32[]{:S(2)}) async-start(bf16[8,504,128]{2,1,0:T(8,128)(2,1)} %lay.1), calls=%async_computation.2 | async-start | bytes 2064384 | tf_op jit(solution)/shard_map/all_to_all | solution.py:620
  70.4 0.0 copy-done.3
  70.4 0.2 reshape.23
  70.6 1.0 copy.15.pair_ref
  71.6 6.9 %shard_map.64.fine_ref = bf16[5,4,128,1280]{3,2,1,0:T(8,128)(2,1)} custom-call(s32[5,128,1]{2,1,0:T(8,128)S(1)} %copy.15.pair_ref), custom_call_target="tpu_custom_call" | custom-call | flops 32768000 | bytes 6553600 | tf_op jit(solution)/shard_map/pallas_call | solution.py:265
  78.6 0.6 copy.12
  79.2 6.0 %all-to-all-done.2.moved_ref = bf16[8,504,128]{2,1,0:T(8,128)(2,1)S(1)} async-done(((bf16[8,504,128]{2,1,0:T(8,128)(2,1)}), bf16[8,504,128]{2,1,0:T(8,128)(2,1)S(1)}, u32[]{:S(2)}, u32[]{:S(2)}) %all-to-all-start.2) | async-done | bytes 1032224 | tf_op jit(solution)/shard_map/all_to_all | solution.py:620
  85.2 6.4 %unpack.1.heat_ref = bf16[80,1280]{1,0:T(8,128)(2,1)S(1)} custom-call(bf16[8,160,128]{2,1,0:T(8,128)(2,1)S(1)} %bitcast.14, bf16[8,504,128]{2,1,0:T(8,128)(2,1)S(1)} %all-to-all-done.2.moved_ref), custom_call_target="tpu_custom_call" | custom-call | tf_op jit(solution)/shard_map/unpack/pallas_call | solution.py:354
  91.6 7.8 %forward.1 = bf16[128,8,400]{2,1,0:T(8,128)(2,1)} custom-call(bf16[80,1280]{1,0:T(8,128)(2,1)S(1)} %unpack.1.heat_ref, bf16[8,504,128]{2,1,0:T(8,128)(2,1)S(1)} %all-to-all-done.2.moved_ref, bf16[5,4,128,1280]{3,2,1,0:T(8,128)(2,1)} %shard_map.64.fine_ref, s32[5,128,1]{2,1,0:T(8,128)S(1)} %copy.15.pair_ref, s32[1,256]{1,0:T(1,128)S(1)} %bitcast.15), custom_call_target="tpu_custom_call" | custom-call | tf_op jit(solution)/shard_map/forward/pallas_call | solution.py:428
  99.5 4.4 %all-to-all-start.3 = ((bf16[128,8,400]{2,1,0:T(8,128)(2,1)}), bf16[128,8,400]{2,1,0:T(8,128)(2,1)S(1)}, u32[]{:S(2)}, u32[]{:S(2)}) async-start(bf16[128,8,400]{2,1,0:T(8,128)(2,1)} %forward.1), calls=%async_computation.3 | async-start | bytes 2097152 | tf_op jit(solution)/shard_map/all_to_all | solution.py:620
  103.9 0.1 dynamic_slice.3.pair_ref
  104.0 19.1 %all-to-all-done.3.came_ref = bf16[128,8,400]{2,1,0:T(8,128)(2,1)S(1)} async-done(((bf16[128,8,400]{2,1,0:T(8,128)(2,1)}), bf16[128,8,400]{2,1,0:T(8,128)(2,1)S(1)}, u32[]{:S(2)}, u32[]{:S(2)}) %all-to-all-start.3) | async-done | bytes 819232 | tf_op jit(solution)/shard_map/all_to_all | solution.py:620
  123.0 13.2 %legendre.1 = bf16[128,8,400]{2,1,0:T(8,128)(2,1)S(1)} custom-call(s32[5]{0:T(128)S(1)} %dynamic_slice.3.pair_ref, bf16[128,8,400]{2,1,0:T(8,128)(2,1)S(1)} %all-to-all-done.3.came_ref, bf16[5,1344,1280]{2,1,0:T(8,128)(2,1)} %bitcast.16), custom_call_target="tpu_custom_call" | custom-call | tf_op jit(solution)/shard_map/legendre/pallas_call | solution.py:497
  136.2 23.4 %all_to_all.31.came_ref = bf16[128,8,400]{2,1,0:T(8,128)(2,1)S(1)} all-to-all(bf16[128,8,400]{2,1,0:T(8,128)(2,1)S(1)} %legendre.1), channel_id=1, replica_groups=mesh['lat'=16,'lon'=8] {'lat','lon'}, dimensions={0} | all-to-all | bytes 1638400 | tf_op jit(solution)/shard_map/all_to_all | solution.py:620
  159.6 6.9 %inverse.1 = bf16[8,400,128]{2,1,0:T(8,128)(2,1)S(1)} custom-call(bf16[128,8,400]{2,1,0:T(8,128)(2,1)S(1)} %all_to_all.31.came_ref, bf16[5,4,128,1280]{3,2,1,0:T(8,128)(2,1)} %shard_map.64.fine_ref), custom_call_target="tpu_custom_call" | custom-call | tf_op jit(solution)/shard_map/inverse/pallas_call | solution.py:568
  166.5 16.6 %all_to_all.32.came_ref = bf16[8,400,128]{2,1,0:T(8,128)(2,1)S(1)} all-to-all(bf16[8,400,128]{2,1,0:T(8,128)(2,1)S(1)} %inverse.1), channel_id=1, replica_groups=mesh['lat'=16,'lon'=8] {'lon'}, dimensions={0} | all-to-all | bytes 1638400 | tf_op jit(solution)/shard_map/all_to_all | solution.py:620
  183.2 1.4 finish.1
  (8 shorter events, 0.1 us)
Async XLA Ops:
  0.9 1.5 copy-start
  10.7 43.4 %copy-start.1 = (f32[16,80,320]{2,1,0:T(8,128)S(1)}, f32[16,80,320]{2,1,0:T(8,128)}, u32[]{:S(2)}) copy-start(f32[16,80,320]{2,1,0:T(8,128)} %state_ref.3) | copy-start | bytes 4915204
  36.5 33.9 %copy-start.3 = (s32[80]{0:T(128)S(1)}, s32[80]{0:T(128)}, u32[]{:S(2)}) copy-start(s32[80]{0:T(128)} %param.10) | copy-start | bytes 964
  36.5 33.9 %copy-start.2 = (s32[640]{0:T(1024)S(1)}, s32[640]{0:T(1024)}, u32[]{:S(2)}) copy-start(s32[640]{0:T(1024)} %param.9) | copy-start | bytes 7684
  49.5 16.2 %all-to-all-start.1 = ((bf16[128,2,640]{2,1,0:T(2,128)(2,1)}), bf16[128,2,640]{2,1,0:T(2,128)(2,1)S(1)}, u32[]{:S(2)}, u32[]{:S(2)}) async-start(bf16[128,2,640]{2,1,0:T(2,128)(2,1)} %radiate.1), calls=%async_computation.1 | async-start | bytes 655360 | tf_op jit(solution)/shard_map/all_to_all | solution.py:620
  65.7 19.5 %all-to-all-start.2 = ((bf16[8,504,128]{2,1,0:T(8,128)(2,1)}), bf16[8,504,128]{2,1,0:T(8,128)(2,1)S(1)}, u32[]{:S(2)}, u32[]{:S(2)}) async-start(bf16[8,504,128]{2,1,0:T(8,128)(2,1)} %lay.1), calls=%async_computation.2 | async-start | bytes 2064384 | tf_op jit(solution)/shard_map/all_to_all | solution.py:620
  99.5 23.6 %all-to-all-start.3 = ((bf16[128,8,400]{2,1,0:T(8,128)(2,1)}), bf16[128,8,400]{2,1,0:T(8,128)(2,1)S(1)}, u32[]{:S(2)}, u32[]{:S(2)}) async-start(bf16[128,8,400]{2,1,0:T(8,128)(2,1)} %forward.1), calls=%async_computation.3 | async-start | bytes 2097152 | tf_op jit(solution)/shard_map/all_to_all | solution.py:620

commit v3 on v2

--- a/solution.py
+++ b/solution.py
@@ -360,88 +360,86 @@
     )(came, moved)
 
 
-def forward_kernel(nwave, heat_ref, moved_ref, fine_ref, pair_ref, sites_ref, out_ref, rows, mixed):
-    step = pl.program_id(0)
-    devices = pair_ref.shape[1]
+def forward_kernel(
+    nwave, heat_ref, moved_ref, fine_ref, pair_ref, sites_ref, out_ref, held, rows, mixed, sems
+):
+    group, _, devices, half = held.shape
     lines = heat_ref.shape[0]
     cap = lines
 
-    @pl.when(step == 0)
-    def _():
-        rows[...] = jnp.zeros_like(rows)
-        place = iota((256, lines), 0)
-        source = (place // 128) * (lines // 2) + (place % 128) // 2
-        twice = (source == iota((256, lines), 1)) & (place % 128 < lines)
-        double = mm(twice.astype(F32).astype(BF16), heat_ref[...]).astype(BF16)
-        wide = (iota((128, 256), 1) // 2 == iota((128, 256), 0)).astype(F32).astype(BF16)
-        for t in range(5):
-            near, far = (t, t + 4) if t < 4 else (8, 9)
-            warm = [mm(double[:, m * 128 : (m + 1) * 128], wide) for m in (near, far)]
+    def copy(s):
+        return pltpu.make_async_copy(fine_ref.at[s], held.at[s], sems.at[s])
+
+    for s in range(group):
+        copy(s).start()
+    rows[...] = jnp.zeros_like(rows)
+    place = iota((256, lines), 0)
+    source = (place // 128) * (lines // 2) + (place % 128) // 2
+    twice = (source == iota((256, lines), 1)) & (place % 128 < lines)
+    double = mm(twice.astype(F32).astype(BF16), heat_ref[...]).astype(BF16)
+    wide = (iota((128, 256), 1) // 2 == iota((128, 256), 0)).astype(F32).astype(BF16)
+    for t in range(5):
+        near, far = (t, t + 4) if t < 4 else (8, 9)
+        warm = [mm(double[:, m * 128 : (m + 1) * 128], wide) for m in (near, far)]
+        for level in range(2):
+            at = slice(level * 128, level * 128 + lines)
+            hot = []
+            for m, up in zip((near, far), warm):
+                if m < 8:
+                    first = [(2 * h + level) * lines for h in range(2)]
+                    cold = [moved_ref[m, f : f + lines, :] for f in first]
+                else:
+                    side = slice(level * 64, (level + 1) * 64)
+                    cold = [
+                        moved_ref[4 * (m - 8) + q, 4 * lines : 5 * lines, side]
+                        for q in range(4)
+                    ]
+                cold = jnp.concatenate([c.astype(F32) for c in cold], axis=1)
+                hot.append(cold + up[at, :])
+            span = slice(t * 256, (t + 1) * 256)
+            rows[0, at, span] = (hot[0] + hot[1]).astype(BF16)
+            rows[1, at, span] = (hot[0] - hot[1]).astype(BF16)
+
+    for s in range(group):
+        copy(s).wait()
+        products = [
+            lax.dot_general(
+                held[s, 2 * e : 2 * e + 2].reshape(2 * devices, half),
+                rows[e],
+                NT,
+                preferred_element_type=F32,
+            )
+            for e in range(2)
+        ]
+        pair = pair_ref[s]
+        for k in range(4):
+            wave = jnp.where(pair % 2 == k // 2, pair, nwave - 1 - pair)
+            product = products[k // 2][(k % 2) * devices : (k % 2 + 1) * devices, :]
+            part = jnp.where(2 * wave < sites_ref[...], product, 0.0)
             for level in range(2):
-                at = slice(level * 128, level * 128 + lines)
-                hot = []
-                for m, up in zip((near, far), warm):
-                    if m < 8:
-                        first = [(2 * h + level) * lines for h in range(2)]
-                        cold = [moved_ref[m, f : f + lines, :] for f in first]
-                    else:
-                        side = slice(level * 64, (level + 1) * 64)
-                        cold = [
-                            moved_ref[4 * (m - 8) + q, 4 * lines : 5 * lines, side]
-                            for q in range(4)
-                        ]
-                    cold = jnp.concatenate([c.astype(F32) for c in cold], axis=1)
-                    hot.append(cold + up[at, :])
-                span = slice(t * 256, (t + 1) * 256)
-                rows[0, at, span] = (hot[0] + hot[1]).astype(BF16)
-                rows[1, at, span] = (hot[0] - hot[1]).astype(BF16)
-
-    products = [
-        lax.dot_general(
-            fine_ref[0, 2 * e : 2 * e + 2].reshape(2 * devices, rows.shape[2]),
-            rows[e],
-            NT,
-            preferred_element_type=F32,
+                mixed[s, pl.ds(level * 4 + k, devices, stride=8), :] = part[
+                    :, level * 128 : (level + 1) * 128
+                ]
+        out_ref[:, :, s * cap : (s + 1) * cap] = (
+            mixed[s].reshape(devices, 8, 128)[:, :, :cap].astype(BF16)
         )
-        for e in range(2)
-    ]
-    pair = pair_ref[0]
-    for k in range(4):
-        wave = jnp.where(pair % 2 == k // 2, pair, nwave - 1 - pair)
-        product = products[k // 2][(k % 2) * devices : (k % 2 + 1) * devices, :]
-        part = jnp.where(2 * wave < sites_ref[...], product, 0.0)
-        for level in range(2):
-            mixed[pl.ds(level * 4 + k, devices, stride=8), :] = part[
-                :, level * 128 : (level + 1) * 128
-            ]
-    for k in range(5):
-
-        @pl.when(step == k)
-        def _(k=k):
-            out_ref[:, :, k * cap : (k + 1) * cap] = (
-                mixed[...].reshape(devices, 8, 128)[:, :, :cap].astype(BF16)
-            )
 
 
 def forward(heat, moved, fine, pairs, sites, nwave):
-    group, four, devices, nlon = fine.shape
+    group, _, devices, half = fine.shape
+    vmem = pl.BlockSpec(memory_space=pltpu.VMEM)
     return pl.pallas_call(
         functools.partial(forward_kernel, nwave),
-        grid=(group,),
         out_shape=jax.ShapeDtypeStruct((devices, 8, group * 80), BF16),
-        in_specs=[
-            pl.BlockSpec(heat.shape, lambda s: (0, 0)),
-            pl.BlockSpec(moved.shape, lambda s: (0, 0, 0)),
-            pl.BlockSpec((1, four, devices, nlon), lambda s: (s, 0, 0, 0)),
-            pl.BlockSpec((1, devices, 1), lambda s: (s, 0, 0)),
-            pl.BlockSpec(sites.shape, lambda s: (0, 0)),
-        ],
-        out_specs=pl.BlockSpec((devices, 8, group * 80), lambda s: (0, 0, 0)),
+        in_specs=[vmem, vmem, pl.BlockSpec(memory_space=pltpu.HBM), vmem, vmem],
+        out_specs=vmem,
         scratch_shapes=[
-            pltpu.VMEM((2, 256, nlon), BF16),
-            pltpu.VMEM((devices * 8, 128), F32),
-        ],
-        compiler_params=pltpu.CompilerParams(vmem_limit_bytes=20 * 2**20),
+            pltpu.VMEM(fine.shape, BF16),
+            pltpu.VMEM((2, 256, half), BF16),
+            pltpu.VMEM((group, devices * 8, 128), F32),
+            pltpu.SemaphoreType.DMA((group,)),
+        ],
+        compiler_params=pltpu.CompilerParams(vmem_limit_bytes=24 * 2**20),
         name="forward",
     )(heat, moved, fine, pairs, sites)
 
@@ -514,70 +512,62 @@
     )(pairs, came, basis)
 
 
-def inverse_kernel(came_ref, fine_ref, out_ref, mixed, left, total):
-    step = pl.program_id(0)
-    devices = came_ref.shape[0]
+def inverse_kernel(came_ref, fine_ref, out_ref, held, mixed, left, sems):
+    _, group, _, devices, half = held.shape
     blocks = out_ref.shape[0]
-    for k in range(5):
-
-        @pl.when(step == k)
-        def _(k=k):
-            mixed[:, :80] = (
-                came_ref[:, :, k * 80 : (k + 1) * 80].astype(F32).reshape(devices * 8, 80)
-            )
-
-    for k in range(4):
-        for level in range(2):
-            part = mixed[pl.ds(level * 4 + k, devices, stride=8), :]
-            left[level * 80 : (level + 1) * 80, k * devices : (k + 1) * devices] = part.T[
-                :80, :
-            ].astype(BF16)
-    half = fine_ref.shape[3]
+    wide = 2 * devices
+
+    def copy(e, s):
+        return pltpu.make_async_copy(
+            fine_ref.at[s, pl.ds(2 * e, 2)], held.at[e, s], sems.at[e, s]
+        )
+
     for e in range(2):
-        product = mm(
-            left[:, 2 * e * devices : 2 * (e + 1) * devices],
-            fine_ref[0, 2 * e : 2 * e + 2].reshape(2 * devices, half),
+        for s in range(group):
+            copy(e, s).start()
+    for s in range(group):
+        mixed[s, :, :80] = (
+            came_ref[:, :, s * 80 : (s + 1) * 80].astype(F32).reshape(devices * 8, 80)
         )
-
-        @pl.when(step == 0)
-        def _():
-            total[e] = product
-
-        @pl.when(step > 0)
-        def _():
-            total[e] += product
-
-    @pl.when(step == pl.num_programs(0) - 1)
-    def _():
-        for j in range(blocks):
-            k = j % 4
-            for t in range(3):
-                first = k * 256 + t * 128 if t < 2 else 1024 + k * 64
-                span = slice(first, first + (128 if t < 2 else 64))
-                even, odd = total[0, :, span], total[1, :, span]
-                value = (even + odd if j < 4 else even - odd).astype(BF16)
-                if t < 2:
-                    out_ref[j, t * 160 : (t + 1) * 160, :] = value
-                else:
-                    out_ref[j, 320:, :64] = value[:80]
-                    out_ref[j, 320:, 64:] = value[80:]
+        for k in range(4):
+            for level in range(2):
+                part = mixed[s, pl.ds(level * 4 + k, devices, stride=8), :]
+                first = s * wide + (k % 2) * devices
+                left[k // 2, level * 80 : (level + 1) * 80, first : first + devices] = part.T[
+                    :80, :
+                ].astype(BF16)
+    sums = []
+    for e in range(2):
+        for s in range(group):
+            copy(e, s).wait()
+        sums.append(mm(left[e], held[e].reshape(group * wide, half)))
+    for j in range(blocks):
+        k = j % 4
+        for t in range(3):
+            first = k * 256 + t * 128 if t < 2 else 1024 + k * 64
+            span = slice(first, first + (128 if t < 2 else 64))
+            even, odd = sums[0][:, span], sums[1][:, span]
+            value = (even + odd if j < 4 else even - odd).astype(BF16)
+            if t < 2:
+                out_ref[j, t * 160 : (t + 1) * 160, :] = value
+            else:
+                out_ref[j, 320:, :64] = value[:80]
+                out_ref[j, 320:, 64:] = value[80:]
 
 
 def inverse(came, fine, blocks):
-    group, four, devices, half = fine.shape
+    group, _, devices, half = fine.shape
+    vmem = pl.BlockSpec(memory_space=pltpu.VMEM)
     return pl.pallas_call(
         inverse_kernel,
-        grid=(group,),
         out_shape=jax.ShapeDtypeStruct((blocks, 400, 128), BF16),
-        in_specs=[
-            pl.BlockSpec(came.shape, lambda s: (0, 0, 0)),
-            pl.BlockSpec((1, four, devices, half), lambda s: (s, 0, 0, 0)),
-        ],
-        out_specs=pl.BlockSpec((blocks, 400, 128), lambda s: (0, 0, 0)),
+        in_specs=[vmem, pl.BlockSpec(memory_space=pltpu.HBM)],
+        out_specs=vmem,
         scratch_shapes=[
-            pltpu.VMEM((devices * 8, 128), F32),
-            pltpu.VMEM((160, four * devices), BF16),
-            pltpu.VMEM((2, 160, half), F32),
+            pltpu.VMEM((2, group, 2, devices, half), BF16),
+            pltpu.VMEM((group, devices * 8, 128), F32),
+            pltpu.VMEM((2, 160, group * 2 * devices), BF16),
+            pltpu.SemaphoreType.DMA((2, group)),
         ],
         compiler_params=pltpu.CompilerParams(vmem_limit_bytes=24 * 2**20),
         name="inverse",

time: 185 us -> 181 us (0.978)
  Pallas kernels: 64.9 us -> 60.3 us
    pallas_call x2, Pallas kernels: 14.8 us -> 10.2 us  [the longest x1 5.94 us: forward(): pl.pallas_call(functools.partial(forward_kernel, nwave), out_shape=jax.Sh...]
where the time goes in v3:
time: 181 us; the launch traced here: 180 us
  blocking collectives  64.8 us (36%)
  Pallas kernels  60.3 us (33%)
  waiting for transfers between devices  35.5 us (20%)
  starting transfers between devices  13.7 us (8%)
  local copies, waits for them, and re-layouts  4.67 us (3%)
    all_to_all x3, blocking collectives, swap(): return lax.all_to_all(x, axes, split_axis=0, concat_axis=0, tiled=True)  64.8 us
    all_to_all x3, waiting for transfers between devices, swap(): return lax.all_to_all(x, axes, split_axis=0, concat_axis=0, tiled=True)  35.5 us
    all_to_all x3, starting transfers between devices, swap(): return lax.all_to_all(x, axes, split_axis=0, concat_axis=0, tiled=True)  13.7 us
    pallas_call x1, Pallas kernels, legendre(): pl.pallas_call(functools.partial(legendre_kernel, nwave), in_specs=[pl.Bl...  13.2 us
    pallas_call x1, Pallas kernels, radiate(): pl.pallas_call(radiate_kernel, grid=(lat_size,), out_shape=jax.ShapeDtype...  13 us
    pallas_call x1, Pallas kernels, pack(): pl.pallas_call(pack_kernel, out_shape=(jax.ShapeDtypeStruct((640, levels...  8.05 us
    pallas_call x1, Pallas kernels, table(): pl.pallas_call(functools.partial(kernel, nwave), grid=(group,), out_shape...  6.91 us
    pallas_call x1, Pallas kernels, unpack(): pl.pallas_call(unpack_kernel, out_shape=jax.ShapeDtypeStruct(shape, BF16)...  6.43 us
  transfers between devices with their start and end apart: 3, of which 3 were waited for; matrix products, arithmetic and copies ran while one was open for 1% of the time, Pallas kernels for 4%

profile of v3, /device:TPU:1, one launch (start us, length us, event | category | flops | bytes accessed | tf_op | source)
XLA Modules:
  0.0 180.0 jit_solution(2730847753490250677)
XLA Ops:
  0.0 0.8 reduce
  0.8 0.1 reshape.18
  0.9 0.0 copy-start
  0.9 1.5 copy-done
  2.5 8.0 %pack.1 = (bf16[640,256]{1,0:T(8,128)(2,1)S(1)}, s32[10,8,128]{2,1,0:T(8,128)S(1)}) custom-call(f32[16,80,320]{2,1,0:T(8,128)S(1)} %copy-done, s32[40,256]{1,0:T(8,128)S(1)} %pad.8.owner_ref), custom_call_target="tpu_custom_call" | custom-call | flops 6000000000 | bytes 2000000 | tf_op jit(solution)/shard_map/pack/pallas_call | solution.py:124
  10.5 0.2 copy.9
  10.7 0.0 copy-start.1
  10.7 0.4 reshape.19
  11.2 0.4 copy.11
  11.6 24.8 %all_to_all.30.came_ref = bf16[128,16,80]{2,1,0:T(8,128)(2,1)S(1)} all-to-all(bf16[128,16,80]{2,1,0:T(8,128)(2,1)S(1)} %copy.11), channel_id=1, replica_groups=mesh['lat'=16,'lon'=8] {'lat','lon'}, dimensions={0} | all-to-all | bytes 655360 | tf_op jit(solution)/shard_map/all_to_all | solution.py:610
  36.5 13.0 %radiate.1 = bf16[128,2,640]{2,1,0:T(2,128)(2,1)} custom-call(bf16[128,16,80]{2,1,0:T(8,128)(2,1)S(1)} %all_to_all.30.came_ref, bf16[16,16,10240]{2,1,0:T(8,128)(2,1)} %bitcast.17), custom_call_target="tpu_custom_call" | custom-call | tf_op jit(solution)/shard_map/radiate/pallas_call | solution.py:181
  49.5 4.6 %all-to-all-start.1 = ((bf16[128,2,640]{2,1,0:T(2,128)(2,1)}), bf16[128,2,640]{2,1,0:T(2,128)(2,1)S(1)}, u32[]{:S(2)}, u32[]{:S(2)}) async-start(bf16[128,2,640]{2,1,0:T(2,128)(2,1)} %radiate.1), calls=%async_computation.1 | async-start | bytes 655360 | tf_op jit(solution)/shard_map/all_to_all | solution.py:610
  54.1 0.0 copy-done.1
  54.1 1.1 lay.1
  55.3 10.5 %all-to-all-done.1 = bf16[128,2,640]{2,1,0:T(2,128)(2,1)S(1)} async-done(((bf16[128,2,640]{2,1,0:T(2,128)(2,1)}), bf16[128,2,640]{2,1,0:T(2,128)(2,1)S(1)}, u32[]{:S(2)}, u32[]{:S(2)}) %all-to-all-start.1) | async-done | bytes 327712 | tf_op jit(solution)/shard_map/all_to_all | solution.py:610
  65.7 4.7 %all-to-all-start.2 = ((bf16[8,504,128]{2,1,0:T(8,128)(2,1)}), bf16[8,504,128]{2,1,0:T(8,128)(2,1)S(1)}, u32[]{:S(2)}, u32[]{:S(2)}) async-start(bf16[8,504,128]{2,1,0:T(8,128)(2,1)} %lay.1), calls=%async_computation.2 | async-start | bytes 2064384 | tf_op jit(solution)/shard_map/all_to_all | solution.py:610
  70.4 0.0 copy-done.3
  70.4 0.2 reshape.23
  70.6 1.0 copy.15.pair_ref
  71.6 6.9 %shard_map.64.fine_ref = bf16[5,4,128,1280]{3,2,1,0:T(8,128)(2,1)} custom-call(s32[5,128,1]{2,1,0:T(8,128)S(1)} %copy.15.pair_ref), custom_call_target="tpu_custom_call" | custom-call | flops 32768000 | bytes 6553600 | tf_op jit(solution)/shard_map/pallas_call | solution.py:265
  78.6 0.6 copy.12
  79.2 6.0 %all-to-all-done.2.moved_ref = bf16[8,504,128]{2,1,0:T(8,128)(2,1)S(1)} async-done(((bf16[8,504,128]{2,1,0:T(8,128)(2,1)}), bf16[8,504,128]{2,1,0:T(8,128)(2,1)S(1)}, u32[]{:S(2)}, u32[]{:S(2)}) %all-to-all-start.2) | async-done | bytes 1032224 | tf_op jit(solution)/shard_map/all_to_all | solution.py:610
  85.2 6.4 %unpack.1.heat_ref = bf16[80,1280]{1,0:T(8,128)(2,1)S(1)} custom-call(bf16[8,160,128]{2,1,0:T(8,128)(2,1)S(1)} %bitcast.14, bf16[8,504,128]{2,1,0:T(8,128)(2,1)S(1)} %all-to-all-done.2.moved_ref), custom_call_target="tpu_custom_call" | custom-call | tf_op jit(solution)/shard_map/unpack/pallas_call | solution.py:354
  91.6 5.9 %forward.1 = bf16[128,8,400]{2,1,0:T(8,128)(2,1)} custom-call(bf16[80,1280]{1,0:T(8,128)(2,1)S(1)} %unpack.1.heat_ref, bf16[8,504,128]{2,1,0:T(8,128)(2,1)S(1)} %all-to-all-done.2.moved_ref, bf16[5,4,128,1280]{3,2,1,0:T(8,128)(2,1)} %shard_map.64.fine_ref, s32[5,128,1]{2,1,0:T(8,128)S(1)} %copy.15.pair_ref, s32[1,256]{1,0:T(1,128)S(1)} %bitcast.15), custom_call_target="tpu_custom_call" | custom-call | tf_op jit(solution)/shard_map/forward/pallas_call | solution.py:431
  97.6 4.4 %all-to-all-start.3 = ((bf16[128,8,400]{2,1,0:T(8,128)(2,1)}), bf16[128,8,400]{2,1,0:T(8,128)(2,1)S(1)}, u32[]{:S(2)}, u32[]{:S(2)}) async-start(bf16[128,8,400]{2,1,0:T(8,128)(2,1)} %forward.1), calls=%async_computation.3 | async-start | bytes 2097152 | tf_op jit(solution)/shard_map/all_to_all | solution.py:610
  102.0 0.1 dynamic_slice.3.pair_ref
  102.1 19.1 %all-to-all-done.3.came_ref = bf16[128,8,400]{2,1,0:T(8,128)(2,1)S(1)} async-done(((bf16[128,8,400]{2,1,0:T(8,128)(2,1)}), bf16[128,8,400]{2,1,0:T(8,128)(2,1)S(1)}, u32[]{:S(2)}, u32[]{:S(2)}) %all-to-all-start.3) | async-done | bytes 819232 | tf_op jit(solution)/shard_map/all_to_all | solution.py:610
  121.2 13.2 %legendre.1 = bf16[128,8,400]{2,1,0:T(8,128)(2,1)S(1)} custom-call(s32[5]{0:T(128)S(1)} %dynamic_slice.3.pair_ref, bf16[128,8,400]{2,1,0:T(8,128)(2,1)S(1)} %all-to-all-done.3.came_ref, bf16[5,1344,1280]{2,1,0:T(8,128)(2,1)} %bitcast.16), custom_call_target="tpu_custom_call" | custom-call | tf_op jit(solution)/shard_map/legendre/pallas_call | solution.py:495
  134.3 23.4 %all_to_all.31.came_ref = bf16[128,8,400]{2,1,0:T(8,128)(2,1)S(1)} all-to-all(bf16[128,8,400]{2,1,0:T(8,128)(2,1)S(1)} %legendre.1), channel_id=1, replica_groups=mesh['lat'=16,'lon'=8] {'lat','lon'}, dimensions={0} | all-to-all | bytes 1638400 | tf_op jit(solution)/shard_map/all_to_all | solution.py:610
  157.7 4.3 %inverse.1 = bf16[8,400,128]{2,1,0:T(8,128)(2,1)S(1)} custom-call(bf16[128,8,400]{2,1,0:T(8,128)(2,1)S(1)} %all_to_all.31.came_ref, bf16[5,4,128,1280]{3,2,1,0:T(8,128)(2,1)} %shard_map.64.fine_ref), custom_call_target="tpu_custom_call" | custom-call | tf_op jit(solution)/shard_map/inverse/pallas_call | solution.py:561
  162.0 16.6 %all_to_all.32.came_ref = bf16[8,400,128]{2,1,0:T(8,128)(2,1)S(1)} all-to-all(bf16[8,400,128]{2,1,0:T(8,128)(2,1)S(1)} %inverse.1), channel_id=1, replica_groups=mesh['lat'=16,'lon'=8] {'lon'}, dimensions={0} | all-to-all | bytes 1638400 | tf_op jit(solution)/shard_map/all_to_all | solution.py:610
  178.7 1.4 finish.1
  (8 shorter events, 0.1 us)
Async XLA Ops:
  0.9 1.5 copy-start
  10.7 43.4 %copy-start.1 = (f32[16,80,320]{2,1,0:T(8,128)S(1)}, f32[16,80,320]{2,1,0:T(8,128)}, u32[]{:S(2)}) copy-start(f32[16,80,320]{2,1,0:T(8,128)} %state_ref.3) | copy-start | bytes 4915204
  36.5 33.9 %copy-start.3 = (s32[80]{0:T(128)S(1)}, s32[80]{0:T(128)}, u32[]{:S(2)}) copy-start(s32[80]{0:T(128)} %param.10) | copy-start | bytes 964
  36.5 33.9 %copy-start.2 = (s32[640]{0:T(1024)S(1)}, s32[640]{0:T(1024)}, u32[]{:S(2)}) copy-start(s32[640]{0:T(1024)} %param.9) | copy-start | bytes 7684
  49.5 16.2 %all-to-all-start.1 = ((bf16[128,2,640]{2,1,0:T(2,128)(2,1)}), bf16[128,2,640]{2,1,0:T(2,128)(2,1)S(1)}, u32[]{:S(2)}, u32[]{:S(2)}) async-start(bf16[128,2,640]{2,1,0:T(2,128)(2,1)} %radiate.1), calls=%async_computation.1 | async-start | bytes 655360 | tf_op jit(solution)/shard_map/all_to_all | solution.py:610
  65.7 19.5 %all-to-all-start.2 = ((bf16[8,504,128]{2,1,0:T(8,128)(2,1)}), bf16[8,504,128]{2,1,0:T(8,128)(2,1)S(1)}, u32[]{:S(2)}, u32[]{:S(2)}) async-start(bf16[8,504,128]{2,1,0:T(8,128)(2,1)} %lay.1), calls=%async_computation.2 | async-start | bytes 2064384 | tf_op jit(solution)/shard_map/all_to_all | solution.py:610
  97.6 23.6 %all-to-all-start.3 = ((bf16[128,8,400]{2,1,0:T(8,128)(2,1)}), bf16[128,8,400]{2,1,0:T(8,128)(2,1)S(1)}, u32[]{:S(2)}, u32[]{:S(2)}) async-start(bf16[128,8,400]{2,1,0:T(8,128)(2,1)} %forward.1), calls=%async_computation.3 | async-start | bytes 2097152 | tf_op jit(solution)/shard_map/all_to_all | solution.py:610
